TPU v7x, 256 devices: a whole 4x4x8 slice. The times are simulated.
256 devices in a mesh: dom: 8 (over z), cls: 32 (over x, y, core).
Axes of the slice: x: 4, y: 4, z: 8, core: 2. Of those that a mesh axis runs over, the one named last changes fastest.
Arguments:
- images: bfloat16 [8192, 64, 256], P(('dom', 'cls'))
- references: bfloat16 [512, 64, 256], P('cls')
- ctf_table: float32 [64, 64], replicated, may hold values from 0.2 to 1
- defocus: int32 [8192], P(('dom', 'cls')), may hold values from 0 to 63
- priors: int32 [8192, 8], P(('dom', 'cls')), may hold values from 0 to 511, as said below
Outputs:
- new_refs: float32 [512, 64, 256], P('cls', 'dom')
Inputs may be any that keep to these rules, and one draw needn't show every extreme that they name: `priors`: the owner of class k is index k // 16 of cls. Among the prior entries of one device's particles at most 10 name classes of any one owner; in each index of dom one owner is named exactly 10 times by every device.
All inputs are finite; a program needn't handle non-finite values.
Results may differ from a plain program's by a relative error of at most 0.011.
Values may be sent and summed in bfloat16 or wider, within the bound.
No kernel may reach another device: no remote copies, remote signals or barrier semaphores. Data moves between devices by JAX's collectives and lax.ppermute only.
A program may use at most 128 MiB of HBM per device.

v0:
```python
import math

import jax
import jax.numpy as jnp
from jax import lax
from jax.sharding import PartitionSpec as P


def angle_tables(angles):
    harm_count = angles // 2
    angle_index = jnp.arange(angles, dtype=jnp.int32)
    harm_index = jnp.arange(harm_count, dtype=jnp.int32)
    phase_grid = angle_index[:, None] * harm_index[None, :] % angles
    angle_grid = 2.0 * jnp.pi / angles * phase_grid.astype(jnp.float32)
    cosine = jnp.cos(angle_grid)
    sine_grid = jnp.sin(angle_grid)
    forward = jnp.concatenate([cosine, sine_grid], axis=1)
    harm_weight = jnp.where(harm_index == 0, 1.0, 2.0).astype(jnp.float32) / angles
    inverse = jnp.concatenate(
        [cosine.T * harm_weight[:, None], -sine_grid.T * harm_weight[:, None]], axis=0
    )
    return (forward, inverse)


def to_harmonics(frames, forward):
    frame_count, cycle_count, angles = frames.shape
    flat_rows = jnp.dot(
        frames.reshape(frame_count * cycle_count, angles),
        forward.astype(jnp.bfloat16),
        preferred_element_type=jnp.float32,
    )
    return flat_rows.astype(jnp.bfloat16).reshape(frame_count, cycle_count, forward.shape[1])


def slot_scores(part_block, ref_block, ctf_block, inverse):
    harm_count = part_block.shape[2] // 2
    part_cos = part_block[:, :, :harm_count].astype(jnp.float32)
    part_sin = part_block[:, :, harm_count:].astype(jnp.float32)
    ref_cos = ref_block[:, :, :harm_count].astype(jnp.float32)
    ref_sin = ref_block[:, :, harm_count:].astype(jnp.float32)
    ctf_weight = ctf_block[:, :, None]
    real_part = jnp.sum(ctf_weight * (part_cos * ref_cos + part_sin * ref_sin), axis=1)
    imag_part = jnp.sum(ctf_weight * (part_cos * ref_sin - part_sin * ref_cos), axis=1)
    joined = jnp.concatenate([real_part, imag_part], axis=1)
    return jnp.dot(joined, inverse, precision=lax.Precision.HIGHEST)


def accumulate_terms(part_block, weights, ctf_block, forward):
    harm_count = part_block.shape[2] // 2
    spectrum = jnp.dot(weights, forward, precision=lax.Precision.HIGHEST)
    w_cos = spectrum[:, None, :harm_count]
    w_sin = spectrum[:, None, harm_count:]
    part_cos = part_block[:, :, :harm_count].astype(jnp.float32)
    part_sin = part_block[:, :, harm_count:].astype(jnp.float32)
    ctf_weight = ctf_block[:, :, None]
    real_part = ctf_weight * (part_cos * w_cos + part_sin * w_sin)
    imag_part = ctf_weight * (part_sin * w_cos - part_cos * w_sin)
    term_rows = jnp.concatenate([real_part, imag_part], axis=2)
    norm_rows = ctf_block * ctf_block * jnp.sum(weights, axis=1)[:, None]
    return (term_rows, norm_rows)


def on_device(images, references, ctf_table, defocus, priors):
    owners = lax.axis_size("cls")
    owned = references.shape[0]
    particles = images.shape[0]
    cycle_count = images.shape[1]
    angles = images.shape[2]
    prior_count = priors.shape[1]
    capacity = 5 * particles * prior_count // (4 * owners)
    send_rows = owners * capacity
    forward, inverse = angle_tables(angles)
    classes = priors.reshape(-1)
    target = classes // owned
    local_class = classes - target * owned
    owner_hits = (target[:, None] == jnp.arange(owners, dtype=jnp.int32)[None, :]).astype(jnp.int32)
    earlier = jnp.cumsum(owner_hits, axis=0) - owner_hits
    places = target * capacity + jnp.sum(earlier * owner_hits, axis=1)
    source = jnp.arange(particles * prior_count, dtype=jnp.int32) // prior_count
    class_buffer = jnp.full((send_rows,), -1, jnp.int32).at[places].set(local_class)
    group_buffer = jnp.zeros((send_rows,), jnp.int32).at[places].set(defocus[source])
    harmonic = to_harmonics(images, forward)
    payload = (
        jnp.zeros((send_rows, cycle_count, harmonic.shape[2]), jnp.bfloat16)
        .at[places]
        .set(harmonic[source])
    )
    received, got_class, got_group = (
        lax.all_to_all(payload, "cls", split_axis=0, concat_axis=0, tiled=True),
        lax.all_to_all(class_buffer, "cls", split_axis=0, concat_axis=0, tiled=True),
        lax.all_to_all(group_buffer, "cls", split_axis=0, concat_axis=0, tiled=True),
    )
    ref_harm = to_harmonics(references, forward)
    group_total = ctf_table.shape[0]
    group_hits = (got_group[:, None] == jnp.arange(group_total, dtype=jnp.int32)[None, :]).astype(
        jnp.float32
    )
    ctf_rows = jnp.dot(group_hits, ctf_table, precision=lax.Precision.HIGHEST)
    filled = got_class >= 0
    class_index = jnp.maximum(got_class, 0)
    block_rows = math.gcd(64, send_rows)
    block_count = send_rows // block_rows
    part_blocks = received.reshape(block_count, block_rows, cycle_count, received.shape[2])
    pick_blocks = class_index.reshape(block_count, block_rows)
    ctf_blocks = ctf_rows.reshape(block_count, block_rows, cycle_count)

    def score_block(inputs):
        part_block, pick_block, ctf_block = inputs
        return slot_scores(part_block, jnp.take(ref_harm, pick_block, axis=0), ctf_block, inverse)

    scores = lax.map(score_block, (part_blocks, pick_blocks, ctf_blocks)).reshape(send_rows, angles)
    returned = lax.all_to_all(scores, "cls", split_axis=0, concat_axis=0, tiled=True)
    grouped = returned[places].reshape(particles, prior_count * angles)
    highest = jnp.max(grouped, axis=1, keepdims=True)
    log_total = highest + jnp.log(jnp.sum(jnp.exp(grouped - highest), axis=1, keepdims=True))
    normal_buffer = (
        jnp.zeros((send_rows,), jnp.float32)
        .at[places]
        .set(jnp.repeat(log_total.reshape(-1), prior_count))
    )
    got_log = lax.all_to_all(normal_buffer, "cls", split_axis=0, concat_axis=0, tiled=True)
    weights = jnp.where(filled[:, None], jnp.exp(scores - got_log[:, None]), 0.0)
    weight_blocks = weights.reshape(block_count, block_rows, angles)
    live_blocks = filled.reshape(block_count, block_rows)
    class_range = jnp.arange(owned, dtype=jnp.int32)

    def add_block(carry, inputs):
        class_sums, class_norms = carry
        part_block, pick_block, ctf_block, block_weights, live_block = inputs
        term_rows, norm_rows = accumulate_terms(part_block, block_weights, ctf_block, forward)
        member = ((pick_block[:, None] == class_range[None, :]) & live_block[:, None]).astype(
            jnp.float32
        )
        class_sums = class_sums + jnp.dot(
            member.T, term_rows.reshape(block_rows, -1), precision=lax.Precision.HIGHEST
        )
        class_norms = class_norms + jnp.dot(member.T, norm_rows, precision=lax.Precision.HIGHEST)
        return ((class_sums, class_norms), None)

    initial = (
        jnp.zeros((owned, cycle_count * received.shape[2]), jnp.float32),
        jnp.zeros((owned, cycle_count), jnp.float32),
    )
    (class_sums, class_norms), ignored = lax.scan(
        add_block, initial, (part_blocks, pick_blocks, ctf_blocks, weight_blocks, live_blocks)
    )
    part_sums, part_norms = (
        lax.psum_scatter(
            class_sums.reshape(owned, cycle_count, received.shape[2]),
            "dom",
            scatter_dimension=1,
            tiled=True,
        ),
        lax.psum_scatter(class_norms, "dom", scatter_dimension=1, tiled=True),
    )
    return part_sums / (part_norms + 1.0)[:, :, None]


def solution(mesh):
    return jax.shard_map(
        on_device,
        mesh=mesh,
        in_specs=(
            P(("dom", "cls"), None, None),
            P("cls", None, None),
            P(),
            P(("dom", "cls")),
            P(("dom", "cls"), None),
        ),
        out_specs=P("cls", "dom", None),
        check_vma=False,
    )
```

profile of v0, /device:TPU:1, one launch (start us, length us, event | category | flops | bytes accessed | tf_op | source)
XLA Modules:
  0.0 459.1 jit_solution(15620542821259937161)
XLA Ops:
  6.5 2.1 fusion.65
  8.6 1.8 fusion.66
  12.5 20.1 %compare_select_fusion.7 = s32[256]{0:T(256)S(1)} fusion(s32[256]{0:T(256)S(1)} %bitcast.169, s32[]{:T(128)} %bitcast.11, s32[]{:T(128)} %bitcast.12, s32[]{:T(128)} %bitcast.13, s32[]{:T(128)} %bitcast.14, s32[]{:T(128)} %bitcast.15, s32[]{:T(128)} %bitcast.16, s32[]{:T(128)} %bitcast.17, s32[]{:T(128)} %bitcast.18, s32[]{:T(128)} %bitcast.19, ...), kind=kLoop, calls=%fused_computation.123 | loop fusion | flops 15872 | bytes 2176 | tf_op jit(solution)/shard_map/gather | solution.py:81
  34.7 8.6 %all-to-all-start.1 = ((s32[32,10,1]{1,2,0:T(1,128)}), s32[32,10,1]{1,2,0:T(1,128)S(1)}, u32[]{:S(2)}, u32[]{:S(2)}) async-start(s32[32,10,1]{1,2,0:T(1,128)} %bitcast.43), calls=%async_computation.1 | async-start | bytes 32768 | tf_op jit(solution)/shard_map/all_to_all | solution.py:91
  46.4 3.7 all-to-all-done.1
  50.1 4.1 all-to-all-start
  54.7 8.6 %gather_fusion.1 = bf16[256,64,256]{2,1,0:T(8,128)(2,1)} fusion(bf16[32,64,256]{2,1,0:T(8,128)(2,1)S(1)} %bitcast.159, s32[1024]{0:T(1024)S(1)} %pad_clamp_fusion.2), kind=kCustom, calls=%fused_computation.1 | custom fusion | bytes 16778240 | tf_op jit(solution)/shard_map/gather | solution.py:86
  63.4 5.2 %broadcast_in_dim.50 = bf16[320,64,256]{2,1,0:T(8,128)(2,1)} broadcast(bf16[]{:T(256)} %constant.108.clone.1), dimensions={} | broadcast | bytes 10485762 | tf_op jit(solution)/shard_map/broadcast_in_dim | solution.py:84
  68.5 37.2 %scatter_fusion = bf16[320,64,256]{2,1,0:T(8,128)(2,1)} fusion(bf16[320,64,256]{2,1,0:T(8,128)(2,1)} %broadcast_in_dim.50, s32[256]{0:T(256)S(1)} %bitcast.166, bf16[256,64,256]{2,1,0:T(8,128)(2,1)} %gather_fusion.1), kind=kCustom, calls=%fused_computation.5 | custom fusion | bytes 25166848 | tf_op jit(solution)/shard_map/scatter | solution.py:86
  105.8 7.6 %all-to-all-start.2 = ((bf16[320,64,256]{2,1,0:T(8,128)(2,1)}), bf16[320,64,256]{2,1,0:T(8,128)(2,1)}, u32[]{:S(2)}, u32[]{:S(2)}) async-start(bf16[320,64,256]{2,1,0:T(8,128)(2,1)} %scatter_fusion), calls=%async_computation.2 | async-start | bytes 20971520 | tf_op jit(solution)/shard_map/all_to_all | solution.py:89
  116.3 138.1 %all-to-all-done.2 = bf16[320,64,256]{2,1,0:T(8,128)(2,1)} async-done(((bf16[320,64,256]{2,1,0:T(8,128)(2,1)}), bf16[320,64,256]{2,1,0:T(8,128)(2,1)}, u32[]{:S(2)}, u32[]{:S(2)}) %all-to-all-start.2) | async-done | bytes 10485792 | tf_op jit(solution)/shard_map/all_to_all | solution.py:89
  254.5 36.0 %while.25 = (s32[]{:T(128)}, f32[5,64,256]{2,1,0:T(8,128)S(1)}, f32[5,64,64]{2,1,0:T(8,128)S(1)}, bf16[5,64,64,256]{3,2,1,0:T(8,128)(2,1)}, s32[5,64]{1,0:T(8,12...) while((s32[]{:T(128)}, f32[5,64,256]{2,1,0:T(8,128)S(1)}, ...), condition=%wide.region_9.10_spmd.clone, body=%wide.region_6.9_spmd.sunk.clone | while | flops 58721856 | bytes 17290720 | solution.py:111
  254.5 2.0 gather_fusion
  256.5 1.8 broadcast_select_fusion.3
  258.3 1.7 dynamic-slice_bitcast_fusion.16
  261.7 2.0 gather_fusion
  263.7 1.8 broadcast_select_fusion.3
  265.6 1.7 dynamic-slice_bitcast_fusion.16
  268.9 2.0 gather_fusion
  270.9 1.8 broadcast_select_fusion.3
  272.8 1.7 dynamic-slice_bitcast_fusion.16
  276.1 2.0 gather_fusion
  278.1 1.8 broadcast_select_fusion.3
  280.0 1.7 dynamic-slice_bitcast_fusion.16
  283.4 2.0 gather_fusion
  285.3 1.8 broadcast_select_fusion.3
  287.2 1.7 dynamic-slice_bitcast_fusion.16
  291.5 30.4 %all-to-all-start.3 = ((f32[32,10,256]{2,1,0:T(8,128)}), f32[32,10,256]{2,1,0:T(8,128)}, u32[]{:S(2)}, u32[]{:S(2)}) async-start(f32[32,10,256]{2,1,0:T(8,128)} %all_to_all.34), calls=%async_computation.3 | async-start | bytes 1048576 | tf_op jit(solution)/shard_map/all_to_all | solution.py:112
  322.0 11.6 %all-to-all-done.3 = f32[32,10,256]{2,1,0:T(8,128)} async-done(((f32[32,10,256]{2,1,0:T(8,128)}), f32[32,10,256]{2,1,0:T(8,128)}, u32[]{:S(2)}, u32[]{:S(2)}) %all-to-all-start.3) | async-done | bytes 327712 | tf_op jit(solution)/shard_map/all_to_all | solution.py:112
  338.9 3.6 all-to-all-start.4
  342.8 6.6 %all-to-all-done.4 = f32[32,10,1]{1,2,0:T(1,128)S(1)} async-done(((f32[32,10,1]{1,2,0:T(1,128)}), f32[32,10,1]{1,2,0:T(1,128)S(1)}, u32[]{:S(2)}, u32[]{:S(2)}) %all-to-all-start.4) | async-done | bytes 1312 | tf_op jit(solution)/shard_map/all_to_all | solution.py:121
  350.9 64.5 %while.26 = (s32[]{:T(128)}, f32[16,16384]{1,0:T(8,128)S(1)}, f32[16,64]{1,0:T(8,128)S(1)}, s32[5,64]{1,0:T(8,128)S(1)}, pred[5,64]{1,0:T(8,128)(4,1)S(1)}, /*in...) while((s32[]{:T(128)}, f32[16,16384]{1,0:T(8,128)S(1)}, ...), condition=%wide.region_17.18_spmd.clone.clone, body=%wide.region_15.17_spmd.clone.sunk.clone | while | flops 259291072 | bytes 34285436 | solution.py:144
  351.9 1.7 dynamic-slice_bitcast_fusion.18
  355.2 4.5 copy.35
  359.6 3.8 convolution_add_fusion.6
  364.8 1.7 dynamic-slice_bitcast_fusion.18
  368.1 4.5 copy.35
  372.5 3.8 convolution_add_fusion.6
  377.7 1.7 dynamic-slice_bitcast_fusion.18
  381.0 4.5 copy.35
  385.4 3.8 convolution_add_fusion.6
  390.6 1.7 dynamic-slice_bitcast_fusion.18
  393.9 4.5 copy.35
  398.3 3.8 convolution_add_fusion.6
  406.8 4.5 copy.35
  411.2 3.8 convolution_add_fusion.6
  418.0 16.7 %all-reduce = f32[16,64]{1,0:T(8,128)S(1)} all-reduce(f32[16,64]{1,0:T(8,128)S(1)} %get-tuple-element.97), channel_id=3, replica_groups=mesh['dom'=8,'cls'=32] {'dom'}, use_global_device_ids=true, to_apply=%region_19.20.clone | all-reduce | flops 1024 | bytes 8192
  434.8 15.8 %reduce-scatter.3.cloned.1.call-done = f32[16,8,256]{2,1,0:T(8,128)} async-done(((f32[16,64,256]{2,1,0:T(8,128)}), f32[16,8,256]{2,1,0:T(8,128)}) %reduce-scatter.3.cloned.1.call-update) | async-done | bytes 131088 | tf_op jit(solution)/shard_map/reduce_scatter | solution.py:148
  (157 shorter events, 46.4 us)
Async XLA Ops:
  6.5 37.3 %copy-start = (bf16[32,64,256]{2,1,0:T(8,128)(2,1)S(1)}, bf16[32,64,256]{2,1,0:T(8,128)(2,1)}, u32[]{:S(2)}) copy-start(bf16[32,64,256]{2,1,0:T(8,128)(2,1)} %param.9) | copy-start | bytes 3145732
  34.7 15.5 %all-to-all-start.1 = ((s32[32,10,1]{1,2,0:T(1,128)}), s32[32,10,1]{1,2,0:T(1,128)S(1)}, u32[]{:S(2)}, u32[]{:S(2)}) async-start(s32[32,10,1]{1,2,0:T(1,128)} %bitcast.43), calls=%async_computation.1 | async-start | bytes 32768 | tf_op jit(solution)/shard_map/all_to_all | solution.py:91
  50.1 55.7 %all-to-all-start = ((s32[32,10,1]{1,2,0:T(1,128)}), s32[32,10,1]{1,2,0:T(1,128)S(1)}, u32[]{:S(2)}, u32[]{:S(2)}) async-start(s32[32,10,1]{1,2,0:T(1,128)} %bitcast.9), calls=%async_computation | async-start | bytes 32768 | tf_op jit(solution)/shard_map/all_to_all | solution.py:90
  105.8 7.6 %copy-start.4 = (bf16[16,64,256]{2,1,0:T(8,128)(2,1)S(1)}, bf16[16,64,256]{2,1,0:T(8,128)(2,1)}, u32[]{:S(2)}) copy-start(bf16[16,64,256]{2,1,0:T(8,128)(2,1)} %param.10) | copy-start | bytes 1572868
  105.8 148.7 %all-to-all-start.2 = ((bf16[320,64,256]{2,1,0:T(8,128)(2,1)}), bf16[320,64,256]{2,1,0:T(8,128)(2,1)}, u32[]{:S(2)}, u32[]{:S(2)}) async-start(bf16[320,64,256]{2,1,0:T(8,128)(2,1)} %scatter_fusion), calls=%async_computation.2 | async-start | bytes 20971520 | tf_op jit(solution)/shard_map/all_to_all | solution.py:89
  113.4 2.6 copy-start.5
  290.5 1.0 copy-start.1
  290.5 31.4 %copy-start.2 = (f32[5,64,256]{2,1,0:T(8,128)}, f32[5,64,256]{2,1,0:T(8,128)S(1)}, u32[]{:S(2)}) copy-start(f32[5,64,256]{2,1,0:T(8,128)S(1)} %get-tuple-element.95) | copy-start | bytes 983044
  291.5 42.1 %all-to-all-start.3 = ((f32[32,10,256]{2,1,0:T(8,128)}), f32[32,10,256]{2,1,0:T(8,128)}, u32[]{:S(2)}, u32[]{:S(2)}) async-start(f32[32,10,256]{2,1,0:T(8,128)} %all_to_all.34), calls=%async_computation.3 | async-start | bytes 1048576 | tf_op jit(solution)/shard_map/all_to_all | solution.py:112
  333.6 17.1 %copy-start.3 = (f32[5,64,256]{2,1,0:T(8,128)S(1)}, f32[5,64,256]{2,1,0:T(8,128)}, u32[]{:S(2)}) copy-start(f32[5,64,256]{2,1,0:T(8,128)} %copy-done.2) | copy-start | bytes 983044
  338.9 10.5 %all-to-all-start.4 = ((f32[32,10,1]{1,2,0:T(1,128)}), f32[32,10,1]{1,2,0:T(1,128)S(1)}, u32[]{:S(2)}, u32[]{:S(2)}) async-start(f32[32,10,1]{1,2,0:T(1,128)} %bitcast.52), calls=%async_computation.4 | async-start | bytes 32768 | tf_op jit(solution)/shard_map/all_to_all | solution.py:121
  342.5 108.0 %reduce-scatter.3.cloned.1.call-start = ((), (), s32[]{:S(2)}) async-start(), calls=%async_computation.6 | async-start | bytes 1179648 | tf_op jit(solution)/shard_map/reduce_scatter | solution.py:148
  415.4 1.3 copy-start.6
Sparse Core Ops, SparseCore 0:
  416.8 33.6 reduce-scatter.2
where the time goes:
time: 465 us; the launch traced here: 459 us
  waiting for transfers between devices  176 us (38%)
  local copies, waits for them, and re-layouts  124 us (27%)
  starting transfers between devices  54.3 us (12%)
  other arithmetic  49.7 us (11%)
  matrix products  23.8 us (5%)
  blocking collectives  16.7 us (4%)
  between operations  14.5 us (3%)
    all_to_all x1, waiting for transfers between devices, on_device(): lax.all_to_all(payload, 'cls', split_axis=0, concat_axis=0, tiled=True)  138 us
    scatter x1, local copies, waits for them, and re-layouts, on_device(): payload = jnp.zeros((send_rows, cycle_count, harmonic.shape[2]), jnp.bflo...  37.2 us
    all_to_all x1, starting transfers between devices, on_device(): lax.all_to_all(scores, 'cls', split_axis=0, concat_axis=0, tiled=True)  30.4 us
    while x5, local copies, waits for them, and re-layouts  22.3 us
    gather x1, other arithmetic, on_device(): defocus[source]  20.1 us
    dot_general x5, matrix products, add_block(): jnp.dot(member.T, term_rows.reshape(block_rows, -1), precision=lax.Precis...  18.8 us
    squeeze x10, local copies, waits for them, and re-layouts, on_device(): lax.map(score_block, (part_blocks, pick_blocks, ctf_blocks))  17.3 us
    unnamed x1, blocking collectives  16.7 us
  transfers between devices with their start and end apart: 6, of which 5 were waited for; matrix products, arithmetic and copies ran while one was open for 13% of the time, Pallas kernels for 0%

commit v1 on v0

v1 whole, which is shorter than its diff:
```python
import numpy as np

import jax
import jax.numpy as jnp
from jax import lax
from jax.experimental import pallas as pl
from jax.experimental.pallas import tpu as pltpu
from jax.sharding import PartitionSpec as P

F32 = jnp.float32
BF16 = jnp.bfloat16
NT = (((1,), (1,)), ((), ()))
LANES = 128


def tables(angles, slices):
    harm = angles // 2
    per = harm // slices
    s, c, m = np.meshgrid(np.arange(slices), np.arange(2), np.arange(per), indexing="ij")
    harmonic = (s * per + m).reshape(-1)
    is_sin = c.reshape(-1)
    phase = (harmonic[:, None] * np.arange(angles)[None, :]) % angles
    grid = phase * (2.0 * np.pi / angles)
    cosine = np.cos(grid).astype(np.float32)
    sine = np.sin(grid).astype(np.float32)
    forward = np.where(is_sin[:, None] == 0, cosine, sine).astype(np.float32)
    weight = np.where(harmonic == 0, 1.0, 2.0).astype(np.float32) / angles
    inverse = (np.where(is_sin[:, None] == 0, cosine, -sine) * weight[:, None]).T.astype(np.float32)
    column = is_sin * harm + harmonic
    order = np.zeros((angles, angles), np.float32)
    order[np.arange(angles), column] = 1.0
    return forward, inverse, order


def lane_swap(arrays):
    n = len(arrays)
    width = LANES // n
    arrays = list(arrays)
    lane = lax.broadcasted_iota(jnp.int32, arrays[0].shape, 1)
    step = n // 2
    while step >= 1:
        shift = width * step
        low = (lane & shift) == 0
        for a in range(n):
            if a & step == 0:
                x, y = arrays[a], arrays[a + step]
                arrays[a] = jnp.where(low, x, pltpu.roll(y, shift, 1))
                arrays[a + step] = jnp.where(low, pltpu.roll(x, LANES - shift, 1), y)
        step //= 2
    return arrays


def harmonics_kernel(img_ref, ref_ref, pri_ref, def_ref, fwd_ref, out_ref, img_s, ref_s, int_s):
    n, cyc, ang = img_ref.shape
    own = ref_ref.shape[0]
    dest = out_ref.shape[0]
    for k in range(ang // LANES):
        lanes = slice(k * LANES, (k + 1) * LANES)
        img_s[k] = img_ref[:, :, lanes].astype(F32).reshape(n * cyc, LANES)
        ref_s[k] = ref_ref[:, :, lanes].astype(F32).reshape(own * cyc, LANES)
    half = cyc // 2
    fwd = fwd_ref[...]

    def part(src, count, column):
        group = LANES // count
        for c in range(half // group):
            block = jnp.concatenate(
                [
                    jnp.concatenate(
                        [
                            src[k, pl.ds(2 * (group * c + q) + odd, count, stride=cyc), :]
                            for odd in range(2)
                            for q in range(group)
                        ],
                        axis=0,
                    )
                    for k in range(ang // LANES)
                ],
                axis=1,
            ).astype(BF16)
            y = lax.dot_general(fwd, block, NT, preferred_element_type=F32)
            y = y.reshape(dest, 8, 2 * LANES)
            y = jnp.concatenate([y[:, :, :LANES], y[:, :, LANES:]], axis=1)
            out_ref[:, :, column + c * LANES : column + (c + 1) * LANES] = y.astype(BF16)

    part(img_s, n, 0)
    part(ref_s, own, half * n)
    pri = pri_ref[...]
    eye = (
        lax.broadcasted_iota(jnp.int32, (8, 8), 0) == lax.broadcasted_iota(jnp.int32, (8, 8), 1)
    ).astype(F32)
    owner = (pri // own).astype(F32)
    within = (pri - (pri // own) * own).astype(F32)
    int_s[...] = jnp.zeros_like(int_s)
    int_s[0:8, 0:n] = lax.dot_general(eye, owner, NT, preferred_element_type=F32)
    int_s[8:16, 0:n] = lax.dot_general(eye, within, NT, preferred_element_type=F32)
    int_s[0:1, n : 2 * n] = def_ref[...].astype(F32)
    column = half * (n + own)
    out_ref[:, :, column : column + LANES] = jnp.broadcast_to(
        int_s[...].astype(BF16)[None], (dest, 16, LANES)
    )


def one_hot(row, count):
    index = lax.broadcasted_iota(jnp.int32, (count, row.shape[1]), 0)
    return jnp.where(index == row, 1.0, 0.0).astype(BF16)


def flip_rows(x):
    return pltpu.roll(x, 4, x.ndim - 2)


def score_kernel(own, in_ref, ctf_ref, x_ref, cp_ref, cid_ref, c_ref, cq_s, rt_s, x_s):
    src = in_ref.shape[0]
    groups, cyc = ctf_ref.shape
    half = cyc // 2
    total = cp_ref.shape[1]
    n = total // src
    classes = rt_s.shape[1]
    col_r = half * n
    col_i = half * (n + own)
    per = LANES // n
    per_r = LANES // own
    blocks = src // per

    ctf_t = ctf_ref[...].T
    for b in range(blocks):
        lanes = slice(b * LANES, (b + 1) * LANES)
        v = lane_swap(
            [in_ref[per * b + i, :, col_i : col_i + LANES].astype(F32) for i in range(per)]
        )
        cid_ref[:, lanes] = (v[0][0:8] * float(own) + v[0][8:16]).astype(jnp.int32)
        group = v[1][0:1].astype(jnp.int32)
        hot = (lax.broadcasted_iota(jnp.int32, (groups, LANES), 0) == group).astype(F32)
        c_ref[:, lanes] = jnp.dot(
            ctf_t, hot, precision=lax.Precision.HIGHEST, preferred_element_type=F32
        )

    def unpack_r(c, carry):
        col = pl.multiple_of(col_r + c * LANES, LANES)
        for b in range(src // per_r):
            v = lane_swap(
                [in_ref[per_r * b + i, :, pl.ds(col, LANES)].astype(F32) for i in range(per_r)]
            )
            for q in range(per_r):
                row = pl.multiple_of((per_r * c + q) * 16, 16)
                rt_s[pl.ds(row, 16), b * LANES : (b + 1) * LANES] = v[q].astype(BF16)
        return carry

    lax.fori_loop(0, half // per_r, unpack_r, 0)

    upper = lax.broadcasted_iota(jnp.int32, (16, LANES), 0) % 8 >= 4

    def unpack_p(c, carry):
        col = pl.multiple_of(c * LANES, LANES)
        for b in range(blocks):
            lanes = slice(b * LANES, (b + 1) * LANES)
            v = lane_swap(
                [in_ref[per * b + i, :, pl.ds(col, LANES)].astype(F32) for i in range(per)]
            )
            ctf = c_ref[pl.ds(pl.multiple_of(c * 2 * per, 2 * per), 2 * per), lanes]
            for q in range(per):
                row = pl.multiple_of((per * c + q) * 16, 16)
                scale = jnp.concatenate(
                    [
                        jnp.broadcast_to(ctf[2 * q + odd : 2 * q + odd + 1], (8, LANES))
                        for odd in range(2)
                    ],
                    axis=0,
                )
                p = v[q] * scale
                cp_ref[pl.ds(row, 16), lanes] = p
                swapped = flip_rows(p.reshape(2, 8, LANES)).reshape(16, LANES)
                cq_s[pl.ds(row, 16), lanes] = jnp.where(upper, swapped, -swapped)
        return carry

    lax.fori_loop(0, half // per, unpack_p, 0)

    wide = 256
    low = lax.broadcasted_iota(jnp.int32, (8, wide), 0) < 4

    def chunk(t, carry):
        col = pl.multiple_of(t * wide, wide)
        cols = pl.ds(col, wide)
        for j in range(8):
            hot = one_hot(cid_ref[j : j + 1, cols], classes)
            picked = jnp.dot(rt_s[...], hot, preferred_element_type=F32)
            re = jnp.sum((cp_ref[:, cols] * picked).reshape(cyc, 8, wide), axis=0)
            im = jnp.sum((cq_s[:, cols] * picked).reshape(cyc, 8, wide), axis=0)
            x_s[j, :, cols] = jnp.where(low, re + flip_rows(re), im + flip_rows(im))
        return carry

    lax.fori_loop(0, total // wide, chunk, 0)

    for b in range(blocks):
        lanes = slice(b * LANES, (b + 1) * LANES)
        for u in range(8 // per):
            v = lane_swap([x_s[per * u + j, :, lanes] for j in range(per)])
            for i in range(per):
                x_ref[per * b + i, :, u * LANES : (u + 1) * LANES] = v[i]


def weight_kernel(x_ref, inv_ref, fwd_ref, out_ref):
    src, rows, slots = x_ref.shape
    ang = inv_ref.shape[0]
    high = lax.Precision.HIGHEST
    x = x_ref[...].reshape(src * rows, slots)
    score = jnp.dot(inv_ref[...], x, precision=high, preferred_element_type=F32)

    def over_slots(row, op):
        row = op(row[:, :LANES], row[:, LANES:])
        row = op(row, pltpu.roll(row, 64, 1))
        row = op(row, pltpu.roll(row, 32, 1))
        return jnp.concatenate([row, row], axis=1)

    top = jnp.broadcast_to(jnp.max(score, axis=0, keepdims=True), (8, slots))
    top = over_slots(top, jnp.maximum)[0:1]
    grown = jnp.exp(score - top)
    mass = jnp.broadcast_to(jnp.sum(grown, axis=0, keepdims=True), (8, slots))
    mass = over_slots(mass, jnp.add)[0:1]
    weight = grown * (1.0 / mass)
    spectrum = jnp.dot(fwd_ref[...], weight, precision=high, preferred_element_type=F32)
    out_ref[...] = spectrum.reshape(src, rows, slots)


def sum_kernel(w_ref, cp_ref, cid_ref, c_ref, out_ref, w_s, t_s, sum_s):
    src = w_ref.shape[0]
    feats, total = cp_ref.shape
    cyc = c_ref.shape[0]
    classes = out_ref.shape[2]
    doms = out_ref.shape[0]
    n = total // src
    per = LANES // n
    for b in range(src // per):
        lanes = slice(b * LANES, (b + 1) * LANES)
        for u in range(8 // per):
            v = lane_swap(
                [w_ref[per * b + i, :, u * LANES : (u + 1) * LANES] for i in range(per)]
            )
            for j in range(per):
                w_s[per * u + j, :, lanes] = v[j]

    wide = 512
    low = lax.broadcasted_iota(jnp.int32, (8, wide), 0) < 4
    sum_s[...] = jnp.zeros_like(sum_s)

    def step(s, carry):
        j = s // (total // wide)
        col = pl.multiple_of((s % (total // wide)) * wide, wide)
        cols = pl.ds(col, wide)
        w = w_s[j, :, cols]
        turned = flip_rows(w)
        wc = jnp.where(low, w, turned)
        ws = jnp.where(low, turned, -w)
        p = cp_ref[:, cols].reshape(cyc, 8, wide)
        term = p * wc[None] + flip_rows(p) * ws[None]
        c = c_ref[:, cols]
        t_s[0:feats] = term.reshape(feats, wide).astype(BF16)
        t_s[feats : feats + cyc] = (c * c * w[0:1]).astype(BF16)
        hot = one_hot(cid_ref[pl.ds(j, 1), cols], classes)
        sum_s[...] += lax.dot_general(t_s[...], hot, NT, preferred_element_type=F32)
        return carry

    lax.fori_loop(0, 8 * (total // wide), step, 0)
    rows = feats // doms
    part = cyc // doms
    for d in range(doms):
        out_ref[d, 0:rows] = sum_s[d * rows : (d + 1) * rows].astype(BF16)
        out_ref[d, rows : rows + part] = sum_s[
            feats + d * part : feats + (d + 1) * part
        ].astype(BF16)


def regroup_kernel(in_ref, out_ref, s_s):
    doms, rows, classes = in_ref.shape
    s_s[...] = jnp.sum(in_ref[...].astype(F32), axis=0)
    owners = out_ref.shape[0]
    own = classes // owners
    per = LANES // own
    for b in range(classes // LANES):
        lanes = slice(b * LANES, (b + 1) * LANES)
        sums = lane_swap([s_s[8 * q : 8 * q + 8, lanes] for q in range(per)])
        norm = s_s[8 * per : 8 * per + 8, lanes]
        norms = lane_swap([jnp.broadcast_to(norm[q : q + 1], (8, LANES)) for q in range(per)])
        for k in range(per):
            out_ref[per * b + k] = jnp.concatenate([sums[k], norms[k]], axis=0).astype(BF16)


def finish_kernel(in_ref, order_ref, out_ref):
    src = in_ref.shape[0]
    own, part, width = out_ref.shape
    both = in_ref[...].astype(F32)
    x = jnp.concatenate([both[:, 0:8].reshape(src * 8, LANES), both[0, 8:16]], axis=0).astype(BF16)
    a = lax.broadcasted_iota(jnp.int32, (LANES, LANES), 0)
    b = lax.broadcasted_iota(jnp.int32, (LANES, LANES), 1)
    turn = jnp.where((a % own) * part + a // own == b, 1.0, 0.0).astype(BF16)
    x = jnp.dot(x, turn, preferred_element_type=F32)
    sums = x[0 : src * 8].T.astype(BF16)
    sums = jnp.dot(sums, order_ref[...], preferred_element_type=F32)
    norm = x[src * 8 :].T[:, 0:1]
    out_ref[...] = (sums / (norm + 1.0)).reshape(own, part, width)


def call(kernel, shapes, scratch, *args):
    many = isinstance(shapes, (list, tuple)) and not hasattr(shapes, "dtype")
    spec = pl.BlockSpec(memory_space=pltpu.VMEM)
    return pl.pallas_call(
        kernel,
        out_shape=shapes,
        in_specs=[spec] * len(args),
        out_specs=[spec] * len(shapes) if many else spec,
        scratch_shapes=scratch,
        compiler_params=pltpu.CompilerParams(vmem_limit_bytes=48 << 20),
    )(*args)


def on_device(images, references, ctf_table, defocus, priors):
    owners = lax.axis_size("cls")
    doms = lax.axis_size("dom")
    n, cyc, ang = images.shape
    own = references.shape[0]
    total = owners * n
    classes = owners * own
    feats = 8 * cyc
    forward, inverse, order = tables(ang, owners)
    shape = jax.ShapeDtypeStruct

    def exchange(x, axis):
        return lax.all_to_all(x, axis, split_axis=0, concat_axis=0, tiled=True)

    width = (cyc // 2) * (n + own) + LANES
    sent = call(
        harmonics_kernel,
        shape((owners, 16, width), BF16),
        [
            pltpu.VMEM((ang // LANES, n * cyc, LANES), F32),
            pltpu.VMEM((ang // LANES, own * cyc, LANES), F32),
            pltpu.VMEM((16, LANES), F32),
        ],
        images,
        references,
        priors,
        defocus.reshape(1, n),
        jnp.asarray(forward, BF16),
    )
    got = exchange(sent, "cls")
    x, cp, cid, ctf = call(
        lambda *refs: score_kernel(own, *refs),
        [
            shape((owners, 8, 8 * n), F32),
            shape((feats, total), F32),
            shape((8, total), jnp.int32),
            shape((cyc, total), F32),
        ],
        [
            pltpu.VMEM((feats, total), F32),
            pltpu.VMEM((feats, classes), BF16),
            pltpu.VMEM((8, 8, total), F32),
        ],
        got,
        ctf_table,
    )
    x = exchange(x, "cls")
    spectrum = call(
        weight_kernel,
        shape((owners, 8, 8 * n), F32),
        [],
        x,
        jnp.asarray(inverse),
        jnp.asarray(forward),
    )
    spectrum = exchange(spectrum, "cls")
    sums = call(
        sum_kernel,
        shape((doms, feats // doms + cyc // doms, classes), BF16),
        [
            pltpu.VMEM((8, 8, total), F32),
            pltpu.VMEM((feats + cyc, 512), BF16),
            pltpu.VMEM((feats + cyc, classes), F32),
        ],
        spectrum,
        cp,
        cid,
        ctf,
    )
    sums = exchange(sums, "dom")
    parts = call(
        regroup_kernel,
        shape((owners, 16, LANES), BF16),
        [pltpu.VMEM((feats // doms + cyc // doms, classes), F32)],
        sums,
    )
    parts = exchange(parts, "cls")
    return call(
        finish_kernel,
        shape((own, cyc // doms, ang), F32),
        [],
        parts,
        jnp.asarray(order, BF16),
    )


def solution(mesh):
    return jax.shard_map(
        on_device,
        mesh=mesh,
        in_specs=(
            P(("dom", "cls"), None, None),
            P("cls", None, None),
            P(),
            P(("dom", "cls")),
            P(("dom", "cls"), None),
        ),
        out_specs=P("cls", "dom", None),
        check_vma=False,
    )
```

time: 465 us -> 124 us (0.27); the launches traced: 459 us -> 124 us
  waiting for transfers between devices: 176 us -> 0 us
  local copies, waits for them, and re-layouts: 124 us -> 4.61 us
  blocking collectives: 16.7 us -> 96.3 us
  starting transfers between devices: 54.3 us -> 0 us
  other arithmetic: 49.7 us -> 0 us
  matrix products: 23.8 us -> 0 us
  Pallas kernels: 0 us -> 22.7 us
  between operations: 14.5 us -> 0.07 us
    all_to_all x5 -> x0, waiting for transfers between devices: 160 us -> none  [the longest x1 138 us: on_device(): lax.all_to_all(payload, 'cls', split_axis=0, concat_axis=0, tiled=True)]
    all_to_all x0 -> x5, blocking collectives: none -> 96.3 us  [exchange(): return lax.all_to_all(x, axis, split_axis=0, concat_axis=0, tiled=True)]
    all_to_all x5 -> x0, starting transfers between devices: 54.3 us -> none  [the longest x1 30.4 us: on_device(): lax.all_to_all(scores, 'cls', split_axis=0, concat_axis=0, tiled=True)]
    scatter x4 -> x0, local copies, waits for them, and re-layouts: 41.4 us -> none  [the longest x1 37.2 us: on_device(): payload = jnp.zeros((send_rows, cycle_count, harmonic.shape[2]), jnp.bflo...]
    dot_general x23 -> x0, matrix products: 23.8 us -> none  [the longest x5 18.8 us: add_block(): jnp.dot(member.T, term_rows.reshape(block_rows, -1), precision=lax.Precis...]
    gather x9 -> x0, local copies, waits for them, and re-layouts: 23.4 us -> none  [the longest x5 9.88 us: score_block(): jnp.take(ref_harm, pick_block, axis=0)]
    pallas_call x0 -> x6, Pallas kernels: none -> 22.7 us  [call(): pl.pallas_call(kernel, out_shape=shapes, in_specs=[spec] * len(args), out...]
    while x5 -> x0, local copies, waits for them, and re-layouts: 22.3 us -> none
  transfers between devices with their start and end apart: 6 -> 0, of which waited for: 5 -> 0; matrix products, arithmetic and copies ran while one was open for 13% -> 0% of each run, Pallas kernels for 0% -> 0%
where the time goes in v1:
time: 124 us
  blocking collectives  96.3 us (78%)
  Pallas kernels  22.7 us (18%)
  local copies, waits for them, and re-layouts  4.61 us (4%)
    all_to_all x5, blocking collectives, exchange(): return lax.all_to_all(x, axis, split_axis=0, concat_axis=0, tiled=True)  96.3 us
    pallas_call x6, Pallas kernels, call(): pl.pallas_call(kernel, out_shape=shapes, in_specs=[spec] * len(args), out...  22.7 us
    unnamed x17, local copies, waits for them, and re-layouts  4.61 us

profile of v1, /device:TPU:1, one launch (start us, length us, event | category | flops | bytes accessed | tf_op | source)
XLA Modules:
  0.0 123.7 jit_solution(588264314031750607)
XLA Ops:
  0.0 0.8 copy.10.pri_ref
  0.8 0.0 copy-start
  0.8 1.2 copy-done
  2.0 0.0 copy-start.1
  2.0 1.0 copy-done.1
  3.0 0.0 copy-start.5
  3.0 0.9 copy-done.5
  3.9 0.0 copy-start.7
  3.9 0.7 copy-done.7
  4.6 2.4 %shard_map.91 = bf16[32,16,1664]{2,1,0:T(8,128)(2,1)S(1)} custom-call(bf16[32,64,256]{2,1,0:T(8,128)(2,1)S(1)} %copy-done, bf16[16,64,256]{2,1,0:T(8,128)(2,1)S(1)} %copy-done.1, s32[32,8]{1,0:T(8,128)S(1)} %copy.10.pri_ref, s32[1,32]{1,0:T(1,128)S(1)} %bitcast.1, bf16[256,256]{1,0:T(8,128)(2,1)S(1)} %copy-done.5), custom_call_target="tpu_custom_call" | custom-call | tf_op jit(solution)/shard_map/pallas_call | solution.py:307
  7.0 0.0 copy-start.6
  7.0 32.6 %all_to_all.25.refs_0_ = bf16[32,16,1664]{2,1,0:T(8,128)(2,1)S(1)} all-to-all(bf16[32,16,1664]{2,1,0:T(8,128)(2,1)S(1)} %shard_map.91), channel_id=1, replica_groups=mesh['dom'=8,'cls'=32] {'cls'}, dimensions={0} | all-to-all | bytes 3407872 | tf_op jit(solution)/shard_map/all_to_all | solution.py:329
  39.5 0.0 copy-done.6
  39.5 0.0 copy-start.2
  39.5 0.0 copy-start.3
  39.5 8.9 %shard_map.92 = (f32[32,8,256]{2,1,0:T(8,128)S(1)}, f32[512,1024]{1,0:T(8,128)S(1)}, s32[8,1024]{1,0:T(8,128)S(1)}, f32[64,1024]{1,0:T(8,128)S(1)}) custom-call(bf16[32,16,1664]{2,1,0:T(8,128)(2,1)S(1)} %all_to_all.25.refs_0_, f32[64,64]{1,0:T(8,128)S(1)} %copy-done.6), custom_call_target="tpu_custom_call" | custom-call | tf_op jit(solution)/shard_map/pallas_call | solution.py:307
  48.4 12.5 %all_to_all.26.x_ref = f32[32,8,256]{2,1,0:T(8,128)S(1)} all-to-all(f32[32,8,256]{2,1,0:T(8,128)S(1)} %get-tuple-element.9), channel_id=1, replica_groups=mesh['dom'=8,'cls'=32] {'cls'}, dimensions={0} | all-to-all | bytes 524288 | tf_op jit(solution)/shard_map/all_to_all | solution.py:329
  60.9 0.0 copy-done.2
  60.9 0.0 copy-done.3
  60.9 1.5 %shard_map.93 = f32[32,8,256]{2,1,0:T(8,128)S(1)} custom-call(f32[32,8,256]{2,1,0:T(8,128)S(1)} %all_to_all.26.x_ref, f32[256,256]{1,0:T(8,128)S(1)} %copy-done.3, f32[256,256]{1,0:T(8,128)S(1)} %copy-done.2), custom_call_target="tpu_custom_call" | custom-call | tf_op jit(solution)/shard_map/pallas_call | solution.py:307
  62.4 12.5 %all_to_all.27.w_ref = f32[32,8,256]{2,1,0:T(8,128)S(1)} all-to-all(f32[32,8,256]{2,1,0:T(8,128)S(1)} %shard_map.93), channel_id=1, replica_groups=mesh['dom'=8,'cls'=32] {'cls'}, dimensions={0} | all-to-all | bytes 524288 | tf_op jit(solution)/shard_map/all_to_all | solution.py:329
  74.8 8.7 %shard_map.94 = bf16[8,72,512]{2,1,0:T(8,128)(2,1)S(1)} custom-call(f32[32,8,256]{2,1,0:T(8,128)S(1)} %all_to_all.27.w_ref, f32[512,1024]{1,0:T(8,128)S(1)} %get-tuple-element.10.cp_ref, s32[8,1024]{1,0:T(8,128)S(1)} %get-tuple-element.11.cid_ref, f32[64,1024]{1,0:T(8,128)S(1)} %get-tuple-element.12.c_ref), custom_call_target="tpu_custom_call" | custom-call | tf_op jit(solution)/shard_map/pallas_call | solution.py:307
  83.5 0.0 copy-start.4
  83.5 26.8 %all_to_all.28.in_ref = bf16[8,72,512]{2,1,0:T(8,128)(2,1)S(1)} all-to-all(bf16[8,72,512]{2,1,0:T(8,128)(2,1)S(1)} %shard_map.94), channel_id=1, replica_groups=mesh['dom'=8,'cls'=32] {'dom'}, dimensions={0} | all-to-all | bytes 1179648 | tf_op jit(solution)/shard_map/all_to_all | solution.py:329
  110.4 0.3 shard_map.95
  110.7 11.9 %all_to_all.29.in_ref = bf16[32,16,128]{2,1,0:T(8,128)(2,1)S(1)} all-to-all(bf16[32,16,128]{2,1,0:T(8,128)(2,1)S(1)} %shard_map.95), channel_id=1, replica_groups=mesh['dom'=8,'cls'=32] {'cls'}, dimensions={0} | all-to-all | bytes 262144 | tf_op jit(solution)/shard_map/all_to_all | solution.py:329
  122.6 0.0 copy-done.4
  122.6 1.1 shard_map.96
Async XLA Ops:
  0.8 1.2 copy-start
  2.0 1.0 copy-start.1
  3.0 0.9 copy-start.5
  3.9 0.7 copy-start.7
  7.0 32.6 %copy-start.6 = (f32[64,64]{1,0:T(8,128)S(1)}, f32[64,64]{1,0:T(8,128)}, u32[]{:S(2)}) copy-start(f32[64,64]{1,0:T(8,128)} %refs_1_.1) | copy-start | bytes 49156
  39.5 21.4 %copy-start.2 = (f32[256,256]{1,0:T(8,128)S(1)}, f32[256,256]{1,0:T(8,128)}, u32[]{:S(2)}) copy-start(f32[256,256]{1,0:T(8,128)} %constant.10.clone.fwd_ref) | copy-start | bytes 786436
  39.5 21.4 %copy-start.3 = (f32[256,256]{1,0:T(8,128)S(1)}, f32[256,256]{1,0:T(8,128)}, u32[]{:S(2)}) copy-start(f32[256,256]{1,0:T(8,128)} %constant.9.clone.inv_ref) | copy-start | bytes 786436
  83.5 39.1 %copy-start.4 = (bf16[256,256]{1,0:T(8,128)(2,1)S(1)}, bf16[256,256]{1,0:T(8,128)(2,1)}, u32[]{:S(2)}) copy-start(bf16[256,256]{1,0:T(8,128)(2,1)} %constant.11.clone.order_ref) | copy-start | bytes 393220

commit v2 on v1

v2 whole, which is shorter than its diff:
```python
import numpy as np

import jax
import jax.numpy as jnp
from jax import lax
from jax.experimental import pallas as pl
from jax.experimental.pallas import tpu as pltpu
from jax.sharding import PartitionSpec as P

F32 = jnp.float32
BF16 = jnp.bfloat16
NT = (((1,), (1,)), ((), ()))
LANES = 128


def tables(angles, slices):
    harm = angles // 2
    per = harm // slices
    s, c, m = np.meshgrid(np.arange(slices), np.arange(2), np.arange(per), indexing="ij")
    harmonic = (s * per + m).reshape(-1)
    is_sin = c.reshape(-1)
    phase = (harmonic[:, None] * np.arange(angles)[None, :]) % angles
    grid = phase * (2.0 * np.pi / angles)
    cosine = np.cos(grid).astype(np.float32)
    sine = np.sin(grid).astype(np.float32)
    forward = np.where(is_sin[:, None] == 0, cosine, sine).astype(np.float32)
    weight = np.where(harmonic == 0, 1.0, 2.0).astype(np.float32) / angles
    inverse = (np.where(is_sin[:, None] == 0, cosine, -sine) * weight[:, None]).T.astype(np.float32)
    column = is_sin * harm + harmonic
    order = np.zeros((angles, angles), np.float32)
    order[np.arange(angles), column] = 1.0
    return forward, inverse, order


def lane_swap(arrays):
    n = len(arrays)
    width = LANES // n
    arrays = list(arrays)
    lane = lax.broadcasted_iota(jnp.int32, arrays[0].shape, 1)
    step = n // 2
    while step >= 1:
        shift = width * step
        low = (lane & shift) == 0
        for a in range(n):
            if a & step == 0:
                x, y = arrays[a], arrays[a + step]
                arrays[a] = jnp.where(low, x, pltpu.roll(y, shift, 1))
                arrays[a + step] = jnp.where(low, pltpu.roll(x, LANES - shift, 1), y)
        step //= 2
    return arrays


def harmonics_kernel(img_hbm, ref_hbm, pri_hbm, def_hbm, fwd_hbm, out_hbm, *scratch):
    img_ref, ref_ref, pri_ref, def_ref, fwd_ref, out_ref, img_s, ref_s, int_s, sems, out_sems = scratch
    n, cyc, ang = img_ref.shape
    own = ref_ref.shape[0]
    dest = out_ref.shape[0]
    half = cyc // 2
    pieces = 4
    span = cyc // pieces

    def piece(src, dst, k, sem):
        cut = pl.ds(k * span, span)
        return pltpu.make_async_copy(src.at[:, cut, :], dst.at[:, cut, :], sem)

    copies = [
        pltpu.make_async_copy(fwd_hbm, fwd_ref, sems.at[0]),
        pltpu.make_async_copy(pri_hbm, pri_ref, sems.at[1]),
        pltpu.make_async_copy(def_hbm, def_ref, sems.at[2]),
    ]
    refs = [piece(ref_hbm, ref_ref, k, sems.at[3 + k]) for k in range(pieces)]
    imgs = [piece(img_hbm, img_ref, k, sems.at[3 + pieces + k]) for k in range(pieces)]
    for copy in copies[:1] + refs + imgs + copies[1:]:
        copy.start()
    sent = []

    def send(column, width):
        cut = pl.ds(column, width)
        copy = pltpu.make_async_copy(
            out_ref.at[:, :, cut], out_hbm.at[:, :, cut], out_sems.at[len(sent)]
        )
        copy.start()
        sent.append(copy)

    def part(ref, src, count, column, arrivals):
        group = LANES // count
        steps = half // group
        for p in range(pieces):
            arrivals[p].wait()
            for k in range(ang // LANES):
                lanes = slice(k * LANES, (k + 1) * LANES)
                for i in range(count):
                    block = ref[i, p * span : (p + 1) * span, lanes].astype(F32)
                    src[k, i * cyc + p * span : i * cyc + (p + 1) * span] = block
            for c in range(p * steps // pieces, (p + 1) * steps // pieces):
                block = jnp.concatenate(
                    [
                        jnp.concatenate(
                            [
                                src[k, pl.ds(2 * (group * c + q) + odd, count, stride=cyc), :]
                                for odd in range(2)
                                for q in range(group)
                            ],
                            axis=0,
                        )
                        for k in range(ang // LANES)
                    ],
                    axis=1,
                ).astype(BF16)
                y = lax.dot_general(fwd_ref[...], block, NT, preferred_element_type=F32)
                y = y.reshape(dest, 8, 2 * LANES)
                y = jnp.concatenate([y[:, :, :LANES], y[:, :, LANES:]], axis=1)
                out_ref[:, :, column + c * LANES : column + (c + 1) * LANES] = y.astype(BF16)
            width = steps // pieces * LANES
            send(column + p * width, width)

    copies[0].wait()
    part(ref_ref, ref_s, own, half * n, refs)
    part(img_ref, img_s, n, 0, imgs)
    copies[1].wait()
    copies[2].wait()
    pri = pri_ref[...]
    int_s[...] = jnp.zeros_like(int_s)
    int_s[0:8, 0:n] = (pri // own).astype(F32)
    int_s[8:16, 0:n] = (pri - (pri // own) * own).astype(F32)
    int_s[0:1, n : 2 * n] = def_ref[...].astype(F32)
    column = half * (n + own)
    out_ref[:, :, column : column + LANES] = jnp.broadcast_to(
        int_s[...].astype(BF16)[None], (dest, 16, LANES)
    )
    send(column, LANES)
    for copy in sent:
        copy.wait()


def one_hot(row, count):
    index = lax.broadcasted_iota(jnp.int32, (count, row.shape[1]), 0)
    return jnp.where(index == row, 1.0, 0.0).astype(BF16)


def flip_rows(x):
    return pltpu.roll(x, 4, x.ndim - 2)


def score_kernel(own, in_ref, ctf_ref, x_ref, cp_ref, cq_ref, hot_ref, c_ref, cid_s, rt_s, x_s):
    src = in_ref.shape[0]
    groups, cyc = ctf_ref.shape
    half = cyc // 2
    total = cp_ref.shape[1]
    n = total // src
    col_r = half * n
    col_i = half * (n + own)
    per = LANES // n
    per_r = LANES // own
    blocks = src // per

    ctf_t = ctf_ref[...].T
    for b in range(blocks):
        lanes = slice(b * LANES, (b + 1) * LANES)
        v = lane_swap(
            [in_ref[per * b + i, :, col_i : col_i + LANES].astype(F32) for i in range(per)]
        )
        cid_s[:, lanes] = (v[0][0:8] * float(own) + v[0][8:16]).astype(jnp.int32)
        group = v[1][0:1].astype(jnp.int32)
        hot = (lax.broadcasted_iota(jnp.int32, (groups, LANES), 0) == group).astype(F32)
        c_ref[:, lanes] = jnp.dot(
            ctf_t, hot, precision=lax.Precision.HIGHEST, preferred_element_type=F32
        )

    def unpack_r(c, carry):
        col = pl.multiple_of(col_r + c * LANES, LANES)
        for b in range(src // per_r):
            v = lane_swap(
                [in_ref[per_r * b + i, :, pl.ds(col, LANES)].astype(F32) for i in range(per_r)]
            )
            for q in range(per_r):
                row = pl.multiple_of((per_r * c + q) * 16, 16)
                rt_s[pl.ds(row, 16), b * LANES : (b + 1) * LANES] = v[q].astype(BF16)
        return carry

    lax.fori_loop(0, half // per_r, unpack_r, 0)

    upper = lax.broadcasted_iota(jnp.int32, (16, LANES), 0) % 8 >= 4

    def unpack_p(c, carry):
        col = pl.multiple_of(c * LANES, LANES)
        for b in range(blocks):
            lanes = slice(b * LANES, (b + 1) * LANES)
            v = lane_swap(
                [in_ref[per * b + i, :, pl.ds(col, LANES)].astype(F32) for i in range(per)]
            )
            ctf = c_ref[pl.ds(pl.multiple_of(c * 2 * per, 2 * per), 2 * per), lanes]
            for q in range(per):
                row = pl.multiple_of((per * c + q) * 16, 16)
                scale = jnp.concatenate(
                    [
                        jnp.broadcast_to(ctf[2 * q + odd : 2 * q + odd + 1], (8, LANES))
                        for odd in range(2)
                    ],
                    axis=0,
                )
                p = v[q] * scale
                cp_ref[pl.ds(row, 16), lanes] = p
                swapped = flip_rows(p.reshape(2, 8, LANES)).reshape(16, LANES)
                cq_ref[pl.ds(row, 16), lanes] = jnp.where(upper, swapped, -swapped)
        return carry

    lax.fori_loop(0, half // per, unpack_p, 0)

    chunks, classes, wide = hot_ref.shape
    wide = wide // 8
    low = lax.broadcasted_iota(jnp.int32, (8, wide), 0) < 4

    def chunk(t, carry):
        col = pl.multiple_of(t * wide, wide)
        cols = pl.ds(col, wide)
        for j in range(8):
            hot = one_hot(cid_s[j : j + 1, cols], classes)
            hot_ref[t, :, j * wide : (j + 1) * wide] = hot
            picked = jnp.dot(rt_s[...], hot, preferred_element_type=F32)
            re = jnp.sum((cp_ref[:, cols] * picked).reshape(cyc, 8, wide), axis=0)
            im = jnp.sum((cq_ref[:, cols] * picked).reshape(cyc, 8, wide), axis=0)
            x_s[j, :, cols] = jnp.where(low, re + flip_rows(re), im + flip_rows(im))
        return carry

    lax.fori_loop(0, chunks, chunk, 0)

    for b in range(blocks):
        lanes = slice(b * LANES, (b + 1) * LANES)
        for u in range(8 // per):
            v = lane_swap([x_s[per * u + j, :, lanes] for j in range(per)])
            for i in range(per):
                x_ref[per * b + i, :, u * LANES : (u + 1) * LANES] = v[i]


def weight_kernel(x_ref, inv_ref, fwd_ref, out_ref):
    src, rows, slots = x_ref.shape
    high = lax.Precision.HIGHEST
    x = x_ref[...].reshape(src * rows, slots)
    score = jnp.dot(inv_ref[...], x, precision=high, preferred_element_type=F32)

    def over_slots(row, op):
        row = op(row[:, :LANES], row[:, LANES:])
        row = op(row, pltpu.roll(row, 64, 1))
        row = op(row, pltpu.roll(row, 32, 1))
        return jnp.concatenate([row, row], axis=1)

    top = jnp.broadcast_to(jnp.max(score, axis=0, keepdims=True), (8, slots))
    top = over_slots(top, jnp.maximum)[0:1]
    grown = jnp.exp(score - top)
    part = jnp.broadcast_to(jnp.sum(grown, axis=0, keepdims=True), (8, slots))
    inverse = 1.0 / over_slots(part, jnp.add)
    weight = grown * inverse[0:1]
    spectrum = jnp.dot(fwd_ref[...], weight, precision=high, preferred_element_type=F32)
    out_ref[...] = spectrum.reshape(src, rows, slots).astype(out_ref.dtype)


def sum_kernel(w_ref, cp_ref, cq_ref, hot_ref, c_ref, out_ref, w_s, t_s, sum_s):
    src = w_ref.shape[0]
    feats, total = cp_ref.shape
    chunks, classes, wide = hot_ref.shape
    wide = wide // 8
    cyc = feats // 8
    n = total // src
    per = LANES // n
    for b in range(src // per):
        lanes = slice(b * LANES, (b + 1) * LANES)
        for u in range(8 // per):
            v = lane_swap(
                [w_ref[per * b + i, :, u * LANES : (u + 1) * LANES].astype(F32) for i in range(per)]
            )
            for j in range(per):
                w_s[per * u + j, :, lanes] = v[j]

    low = lax.broadcasted_iota(jnp.int32, (8, wide), 0) < 4
    for t in range(chunks):
        cols = slice(t * wide, (t + 1) * wide)
        for j in range(8):
            w = w_s[j, :, cols]
            turned = flip_rows(w)
            wc = jnp.where(low, w, turned)
            ws = jnp.where(low, turned, w)
            p = cp_ref[:, cols].reshape(cyc, 8, wide)
            q = cq_ref[:, cols].reshape(cyc, 8, wide)
            term = p * wc[None] - q * ws[None]
            slot = slice(j * wide, (j + 1) * wide)
            t_s[t % 2, 0:feats, slot] = term.reshape(feats, wide).astype(BF16)
            c = c_ref[:, cols]
            t_s[t % 2, feats:, slot] = (c * c * w[0:1]).astype(BF16)
        part = lax.dot_general(t_s[t % 2], hot_ref[t], NT, preferred_element_type=F32)
        if t == 0:
            sum_s[...] = part
        else:
            sum_s[...] += part
    own = classes // src
    per = LANES // own
    rows = 8 * per
    for d in range(feats // rows):
        for b in range(classes // LANES):
            lanes = slice(b * LANES, (b + 1) * LANES)
            v = lane_swap([sum_s[d * rows + 8 * q : d * rows + 8 * q + 8, lanes] for q in range(per)])
            norm = sum_s[feats + d * per : feats + (d + 1) * per, lanes]
            norm = lane_swap([jnp.broadcast_to(norm[q : q + 1], (8, LANES)) for q in range(per)])
            for k in range(per):
                part = v[k].astype(BF16)
                to = d * src + per * b + k
                for g in range(4):
                    out_ref[to, :, g * LANES : (g + 1) * LANES] = part[2 * g : 2 * g + 2]
                out_ref[to, :, 4 * LANES :] = norm[k][0:2].astype(BF16)


def finish_kernel(in_ref, order_ref, out_ref):
    own, part, width = out_ref.shape
    every = in_ref.shape[0]
    src = width // 8
    x = jnp.zeros((width, LANES), F32)
    for g in range(4):
        rows = in_ref[:, :, g * LANES : (g + 1) * LANES].reshape(2 * every, LANES)
        x += jnp.dot(order_ref[g], rows, preferred_element_type=F32)
    norm = in_ref[0, :, 4 * LANES :].astype(F32)
    for d in range(1, every // src):
        norm += in_ref[d * src, :, 4 * LANES :].astype(F32)
    x = jnp.concatenate([x, jnp.broadcast_to(norm[0:1], (8, LANES))], axis=0)
    a = lax.broadcasted_iota(jnp.int32, (LANES, LANES), 0)
    b = lax.broadcasted_iota(jnp.int32, (LANES, LANES), 1)
    turn = jnp.where((a % own) * part + a // own == b, 1.0, 0.0)
    x = jnp.dot(x, turn, precision=lax.Precision.HIGHEST, preferred_element_type=F32).T
    out_ref[...] = (x[:, :width] / (x[:, width : width + 1] + 1.0)).reshape(own, part, width)


def call(kernel, shapes, scratch, *args, space=pltpu.VMEM, limit=24):
    many = isinstance(shapes, (list, tuple)) and not hasattr(shapes, "dtype")
    spec = pl.BlockSpec(memory_space=space)
    return pl.pallas_call(
        kernel,
        out_shape=shapes,
        in_specs=[pl.BlockSpec(memory_space=space)] * len(args),
        out_specs=[spec] * len(shapes) if many else spec,
        scratch_shapes=scratch,
        compiler_params=pltpu.CompilerParams(vmem_limit_bytes=limit << 20),
    )(*args)


def on_device(images, references, ctf_table, defocus, priors):
    owners = lax.axis_size("cls")
    doms = lax.axis_size("dom")
    n, cyc, ang = images.shape
    own = references.shape[0]
    total = owners * n
    classes = owners * own
    feats = 8 * cyc
    wide = 256
    forward, inverse, order = tables(ang, owners)
    pairs = order.reshape(owners, 4, 2, ang).transpose(1, 3, 0, 2).reshape(4, ang, 2 * owners)
    pairs = np.tile(pairs, (1, 1, doms))
    shape = jax.ShapeDtypeStruct
    pri = priors.T
    group = defocus.reshape(1, n)

    def exchange(x, axis):
        return lax.all_to_all(x, axis, split_axis=0, concat_axis=0, tiled=True)

    width = (cyc // 2) * (n + own) + LANES
    sent = call(
        harmonics_kernel,
        shape((owners, 16, width), BF16),
        [
            pltpu.VMEM((n, cyc, ang), BF16),
            pltpu.VMEM((own, cyc, ang), BF16),
            pltpu.VMEM((8, n), jnp.int32),
            pltpu.VMEM((1, n), jnp.int32),
            pltpu.VMEM((ang, ang), BF16),
            pltpu.VMEM((owners, 16, width), BF16),
            pltpu.VMEM((ang // LANES, n * cyc, LANES), F32),
            pltpu.VMEM((ang // LANES, own * cyc, LANES), F32),
            pltpu.VMEM((16, LANES), F32),
            pltpu.SemaphoreType.DMA((11,)),
            pltpu.SemaphoreType.DMA((9,)),
        ],
        images,
        references,
        pri,
        group,
        jnp.asarray(forward, BF16),
        space=pltpu.HBM,
        limit=60,
    )
    got = exchange(sent, "cls")
    x, cp, cq, hot, ctf = call(
        lambda *refs: score_kernel(own, *refs),
        [
            shape((owners, 8, 8 * n), F32),
            shape((feats, total), F32),
            shape((feats, total), F32),
            shape((total // wide, classes, 8 * wide), BF16),
            shape((cyc, total), F32),
        ],
        [
            pltpu.VMEM((8, total), jnp.int32),
            pltpu.VMEM((feats, classes), BF16),
            pltpu.VMEM((8, 8, total), F32),
        ],
        got,
        ctf_table,
    )
    x = exchange(x, "cls")
    spectrum = call(
        weight_kernel,
        shape((owners, 8, 8 * n), BF16),
        [],
        x,
        jnp.asarray(inverse),
        jnp.asarray(forward),
    )
    spectrum = exchange(spectrum, "cls")
    sums = call(
        sum_kernel,
        shape((doms * owners, 2, 5 * LANES), BF16),
        [
            pltpu.VMEM((8, 8, total), F32),
            pltpu.VMEM((2, feats + cyc, 8 * wide), BF16),
            pltpu.VMEM((feats + cyc, classes), F32),
        ],
        spectrum,
        cp,
        cq,
        hot,
        ctf,
    )
    sums = exchange(sums, ("dom", "cls"))
    return call(
        finish_kernel,
        shape((own, cyc // doms, ang), F32),
        [],
        sums,
        jnp.asarray(pairs, BF16),
    )


def solution(mesh):
    return jax.shard_map(
        on_device,
        mesh=mesh,
        in_specs=(
            P(("dom", "cls"), None, None),
            P("cls", None, None),
            P(),
            P(("dom", "cls")),
            P(("dom", "cls"), None),
        ),
        out_specs=P("cls", "dom", None),
        check_vma=False,
    )
```

time: 124 us -> 114 us (0.919)
  blocking collectives: 96.3 us -> 89.9 us
  local copies, waits for them, and re-layouts: 4.61 us -> 0.02 us
  Pallas kernels: 22.7 us -> 24 us
    all_to_all x5 -> x4, blocking collectives: 96.3 us -> 89.9 us  [exchange(): return lax.all_to_all(x, axis, split_axis=0, concat_axis=0, tiled=True)]
    unnamed x17 -> x8, local copies, waits for them, and re-layouts: 4.61 us -> 0.02 us
    pallas_call x6 -> x5, Pallas kernels: 22.7 us -> 24 us  [call(): pl.pallas_call(kernel, out_shape=shapes, in_specs=[pl.BlockSpec(memory_sp...]
where the time goes in v2:
time: 114 us
  blocking collectives  89.9 us (79%)
  Pallas kernels  24 us (21%)
    all_to_all x4, blocking collectives, exchange(): return lax.all_to_all(x, axis, split_axis=0, concat_axis=0, tiled=True)  89.9 us
    pallas_call x5, Pallas kernels, call(): pl.pallas_call(kernel, out_shape=shapes, in_specs=[pl.BlockSpec(memory_sp...  24 us

profile of v2, /device:TPU:1, one launch (start us, length us, event | category | flops | bytes accessed | tf_op | source)
XLA Modules:
  0.0 113.9 jit_solution(12356423888754632420)
XLA Ops:
  0.0 5.5 %shard_map.91 = bf16[32,16,1664]{2,1,0:T(8,128)(2,1)} custom-call(bf16[32,64,256]{2,1,0:T(8,128)(2,1)} %img_hbm.1, bf16[16,64,256]{2,1,0:T(8,128)(2,1)} %ref_hbm.1, s32[8,32]{1,0:T(8,128)} %bitcast.2, s32[1,32]{1,0:T(1,128)} %bitcast.3, bf16[256,256]{1,0:T(8,128)(2,1)} %constant.8.clone.fwd_hbm), custom_call_target="tpu_custom_call" | custom-call | tf_op jit(solution)/shard_map/pallas_call | solution.py:334
  5.5 0.0 copy-start.3
  5.6 0.0 copy-start.1
  5.6 0.0 copy-start.2
  5.6 32.9 %all_to_all.20.refs_0_ = bf16[32,16,1664]{2,1,0:T(8,128)(2,1)S(1)} all-to-all(bf16[32,16,1664]{2,1,0:T(8,128)(2,1)} %shard_map.91), channel_id=1, replica_groups=mesh['dom'=8,'cls'=32] {'cls'}, dimensions={0} | all-to-all | bytes 3407872 | tf_op jit(solution)/shard_map/all_to_all | solution.py:361
  38.5 0.0 copy-done.3
  38.5 9.1 %shard_map.92 = (f32[32,8,256]{2,1,0:T(8,128)S(1)}, f32[512,1024]{1,0:T(8,128)S(1)}, f32[512,1024]{1,0:T(8,128)S(1)}, bf16[4,512,2048]{2,1,0:T(8,128)(2,1)S(1)}, f32[64,1024]{1,0:T(8,128)S(1)}) custom-call(bf16[32,16,1664]{2,1,0:T(8,128)(2,1)S(1)} %all_to_all.20.refs_0_, f32[64,64]{1,0:T(8,128)S(1)} %copy-done.3), custom_call_target="tpu_custom_call" | custom-call | tf_op jit(solution)/shard_map/pallas_call | solution.py:334
  47.6 12.5 %all_to_all.21.x_ref = f32[32,8,256]{2,1,0:T(8,128)S(1)} all-to-all(f32[32,8,256]{2,1,0:T(8,128)S(1)} %get-tuple-element.10), channel_id=1, replica_groups=mesh['dom'=8,'cls'=32] {'cls'}, dimensions={0} | all-to-all | bytes 524288 | tf_op jit(solution)/shard_map/all_to_all | solution.py:361
  60.1 0.0 copy-done.1
  60.1 0.0 copy-done.2
  60.1 1.5 %shard_map.93 = bf16[32,8,256]{2,1,0:T(8,128)(2,1)S(1)} custom-call(f32[32,8,256]{2,1,0:T(8,128)S(1)} %all_to_all.21.x_ref, f32[256,256]{1,0:T(8,128)S(1)} %copy-done.2, f32[256,256]{1,0:T(8,128)S(1)} %copy-done.1), custom_call_target="tpu_custom_call" | custom-call | tf_op jit(solution)/shard_map/pallas_call | solution.py:334
  61.5 11.2 %all_to_all.22.w_ref = bf16[32,8,256]{2,1,0:T(8,128)(2,1)S(1)} all-to-all(bf16[32,8,256]{2,1,0:T(8,128)(2,1)S(1)} %shard_map.93), channel_id=1, replica_groups=mesh['dom'=8,'cls'=32] {'cls'}, dimensions={0} | all-to-all | bytes 262144 | tf_op jit(solution)/shard_map/all_to_all | solution.py:361
  72.7 0.0 copy-start
  72.7 6.3 %shard_map.94 = bf16[256,2,640]{2,1,0:T(2,128)(2,1)S(1)} custom-call(bf16[32,8,256]{2,1,0:T(8,128)(2,1)S(1)} %all_to_all.22.w_ref, f32[512,1024]{1,0:T(8,128)S(1)} %get-tuple-element.11.cp_ref, f32[512,1024]{1,0:T(8,128)S(1)} %get-tuple-element.12.cq_ref, bf16[4,512,2048]{2,1,0:T(8,128)(2,1)S(1)} %get-tuple-element.13.hot_ref, ...), custom_call_target="tpu_custom_call" | custom-call | tf_op jit(solution)/shard_map/pallas_call | solution.py:334
  79.0 33.3 %all_to_all.23.in_ref = bf16[256,2,640]{2,1,0:T(2,128)(2,1)S(1)} all-to-all(bf16[256,2,640]{2,1,0:T(2,128)(2,1)S(1)} %shard_map.94), channel_id=1, replica_groups=mesh['dom'=8,'cls'=32] {'dom','cls'}, dimensions={0} | all-to-all | bytes 1310720 | tf_op jit(solution)/shard_map/all_to_all | solution.py:361
  112.3 0.0 copy-done
  112.3 1.6 %shard_map.95 = f32[16,8,256]{2,1,0:T(8,128)} custom-call(bf16[256,2,640]{2,1,0:T(2,128)(2,1)S(1)} %all_to_all.23.in_ref, bf16[4,256,512]{2,1,0:T(8,128)(2,1)S(1)} %copy-done), custom_call_target="tpu_custom_call" | custom-call | tf_op jit(solution)/shard_map/pallas_call | solution.py:334
Async XLA Ops:
  5.5 32.9 %copy-start.3 = (f32[64,64]{1,0:T(8,128)S(1)}, f32[64,64]{1,0:T(8,128)}, u32[]{:S(2)}) copy-start(f32[64,64]{1,0:T(8,128)} %refs_1_.1) | copy-start | bytes 49156
  5.6 54.5 %copy-start.1 = (f32[256,256]{1,0:T(8,128)S(1)}, f32[256,256]{1,0:T(8,128)}, u32[]{:S(2)}) copy-start(f32[256,256]{1,0:T(8,128)} %constant.10.clone.fwd_ref) | copy-start | bytes 786436
  5.6 54.5 %copy-start.2 = (f32[256,256]{1,0:T(8,128)S(1)}, f32[256,256]{1,0:T(8,128)}, u32[]{:S(2)}) copy-start(f32[256,256]{1,0:T(8,128)} %constant.9.clone.inv_ref) | copy-start | bytes 786436
  72.7 39.6 %copy-start = (bf16[4,256,512]{2,1,0:T(8,128)(2,1)S(1)}, bf16[4,256,512]{2,1,0:T(8,128)(2,1)}, u32[]{:S(2)}) copy-start(bf16[4,256,512]{2,1,0:T(8,128)(2,1)} %constant.11.clone.order_ref) | copy-start | bytes 3145732

commit v3 on v2

--- a/solution.py
+++ b/solution.py
@@ -50,92 +50,64 @@
     return arrays
 
 
-def harmonics_kernel(img_hbm, ref_hbm, pri_hbm, def_hbm, fwd_hbm, out_hbm, *scratch):
-    img_ref, ref_ref, pri_ref, def_ref, fwd_ref, out_ref, img_s, ref_s, int_s, sems, out_sems = scratch
+def harmonics_kernel(img_hbm, ref_hbm, pri_hbm, def_hbm, fwd_hbm, out_ref, *scratch):
+    img_ref, ref_ref, pri_ref, def_ref, fwd_ref, img_s, ref_s, int_s, sems = scratch
     n, cyc, ang = img_ref.shape
     own = ref_ref.shape[0]
     dest = out_ref.shape[0]
-    half = cyc // 2
-    pieces = 4
-    span = cyc // pieces
-
-    def piece(src, dst, k, sem):
-        cut = pl.ds(k * span, span)
-        return pltpu.make_async_copy(src.at[:, cut, :], dst.at[:, cut, :], sem)
-
-    copies = [
-        pltpu.make_async_copy(fwd_hbm, fwd_ref, sems.at[0]),
-        pltpu.make_async_copy(pri_hbm, pri_ref, sems.at[1]),
-        pltpu.make_async_copy(def_hbm, def_ref, sems.at[2]),
-    ]
-    refs = [piece(ref_hbm, ref_ref, k, sems.at[3 + k]) for k in range(pieces)]
-    imgs = [piece(img_hbm, img_ref, k, sems.at[3 + pieces + k]) for k in range(pieces)]
-    for copy in copies[:1] + refs + imgs + copies[1:]:
+    pairs = (
+        (fwd_hbm, fwd_ref),
+        (ref_hbm, ref_ref),
+        (img_hbm, img_ref),
+        (pri_hbm, pri_ref),
+        (def_hbm, def_ref),
+    )
+    copies = [pltpu.make_async_copy(a, b, sems.at[k]) for k, (a, b) in enumerate(pairs)]
+    for copy in copies:
         copy.start()
-    sent = []
-
-    def send(column, width):
-        cut = pl.ds(column, width)
-        copy = pltpu.make_async_copy(
-            out_ref.at[:, :, cut], out_hbm.at[:, :, cut], out_sems.at[len(sent)]
-        )
-        copy.start()
-        sent.append(copy)
-
-    def part(ref, src, count, column, arrivals):
-        group = LANES // count
-        steps = half // group
-        for p in range(pieces):
-            arrivals[p].wait()
-            for k in range(ang // LANES):
-                lanes = slice(k * LANES, (k + 1) * LANES)
-                for i in range(count):
-                    block = ref[i, p * span : (p + 1) * span, lanes].astype(F32)
-                    src[k, i * cyc + p * span : i * cyc + (p + 1) * span] = block
-            for c in range(p * steps // pieces, (p + 1) * steps // pieces):
-                block = jnp.concatenate(
-                    [
-                        jnp.concatenate(
-                            [
-                                src[k, pl.ds(2 * (group * c + q) + odd, count, stride=cyc), :]
-                                for odd in range(2)
-                                for q in range(group)
-                            ],
-                            axis=0,
-                        )
-                        for k in range(ang // LANES)
-                    ],
-                    axis=1,
-                ).astype(BF16)
-                y = lax.dot_general(fwd_ref[...], block, NT, preferred_element_type=F32)
-                y = y.reshape(dest, 8, 2 * LANES)
-                y = jnp.concatenate([y[:, :, :LANES], y[:, :, LANES:]], axis=1)
-                out_ref[:, :, column + c * LANES : column + (c + 1) * LANES] = y.astype(BF16)
-            width = steps // pieces * LANES
-            send(column + p * width, width)
-
+
+    def part(ref, src, count, column):
+        for k in range(ang // LANES):
+            src[k] = ref[:, :, k * LANES : (k + 1) * LANES].astype(F32).reshape(count * cyc, LANES)
+        wide = 2 * LANES
+        group = wide // count
+        for c in range(cyc // group):
+            block = jnp.concatenate(
+                [
+                    jnp.concatenate(
+                        [src[k, pl.ds(group * c + q, count, stride=cyc), :] for q in range(group)],
+                        axis=0,
+                    )
+                    for k in range(ang // LANES)
+                ],
+                axis=1,
+            ).astype(BF16)
+            y = lax.dot_general(fwd_ref[...], block, NT, preferred_element_type=F32)
+            cut = slice(column + c * wide, column + (c + 1) * wide)
+            out_ref[:, :, cut] = y.reshape(dest, 8, wide).astype(BF16)
+
+    copies[3].wait()
+    copies[4].wait()
+    int_s[...] = jnp.zeros_like(int_s)
+    int_s[:, 0:n] = (pri_ref[...] - dest * own // 2).astype(F32)
+    int_s[0:1, n : 2 * n] = def_ref[...].astype(F32)
+    column = cyc * (n + own)
+    out_ref[:, :, column : column + LANES] = jnp.broadcast_to(
+        int_s[...].astype(BF16)[None], (dest, 8, LANES)
+    )
     copies[0].wait()
-    part(ref_ref, ref_s, own, half * n, refs)
-    part(img_ref, img_s, n, 0, imgs)
     copies[1].wait()
+    part(ref_ref, ref_s, own, cyc * n)
     copies[2].wait()
-    pri = pri_ref[...]
-    int_s[...] = jnp.zeros_like(int_s)
-    int_s[0:8, 0:n] = (pri // own).astype(F32)
-    int_s[8:16, 0:n] = (pri - (pri // own) * own).astype(F32)
-    int_s[0:1, n : 2 * n] = def_ref[...].astype(F32)
-    column = half * (n + own)
-    out_ref[:, :, column : column + LANES] = jnp.broadcast_to(
-        int_s[...].astype(BF16)[None], (dest, 16, LANES)
-    )
-    send(column, LANES)
-    for copy in sent:
-        copy.wait()
+    part(img_ref, img_s, n, 0)
 
 
 def one_hot(row, count):
-    index = lax.broadcasted_iota(jnp.int32, (count, row.shape[1]), 0)
-    return jnp.where(index == row, 1.0, 0.0).astype(BF16)
+    wide = row.shape[1]
+    index = lax.broadcasted_iota(jnp.int32, (count, wide), 0).astype(jnp.int16)
+    row = jnp.broadcast_to(row, (16, wide)).astype(jnp.int16)
+    hot = index.reshape(count // 16, 16, wide) == row[None]
+    return jnp.where(hot, jnp.ones((), BF16), jnp.zeros((), BF16)).reshape(count, wide)
 
 
 def flip_rows(x):
@@ -145,11 +117,10 @@
 def score_kernel(own, in_ref, ctf_ref, x_ref, cp_ref, cq_ref, hot_ref, c_ref, cid_s, rt_s, x_s):
     src = in_ref.shape[0]
     groups, cyc = ctf_ref.shape
-    half = cyc // 2
     total = cp_ref.shape[1]
     n = total // src
-    col_r = half * n
-    col_i = half * (n + own)
+    col_r = cyc * n
+    col_i = cyc * (n + own)
     per = LANES // n
     per_r = LANES // own
     blocks = src // per
@@ -160,7 +131,7 @@
         v = lane_swap(
             [in_ref[per * b + i, :, col_i : col_i + LANES].astype(F32) for i in range(per)]
         )
-        cid_s[:, lanes] = (v[0][0:8] * float(own) + v[0][8:16]).astype(jnp.int32)
+        cid_s[:, lanes] = v[0].astype(jnp.int32) + src * own // 2
         group = v[1][0:1].astype(jnp.int32)
         hot = (lax.broadcasted_iota(jnp.int32, (groups, LANES), 0) == group).astype(F32)
         c_ref[:, lanes] = jnp.dot(
@@ -173,47 +144,42 @@
             v = lane_swap(
                 [in_ref[per_r * b + i, :, pl.ds(col, LANES)].astype(F32) for i in range(per_r)]
             )
-            for q in range(per_r):
-                row = pl.multiple_of((per_r * c + q) * 16, 16)
-                rt_s[pl.ds(row, 16), b * LANES : (b + 1) * LANES] = v[q].astype(BF16)
+            for q in range(0, per_r, 2):
+                row = pl.multiple_of((per_r * c + q) * 8, 16)
+                pair = jnp.concatenate([v[q], v[q + 1]], axis=0)
+                rt_s[pl.ds(row, 16), b * LANES : (b + 1) * LANES] = pair.astype(BF16)
         return carry
 
-    lax.fori_loop(0, half // per_r, unpack_r, 0)
-
-    upper = lax.broadcasted_iota(jnp.int32, (16, LANES), 0) % 8 >= 4
+    lax.fori_loop(0, cyc // per_r, unpack_r, 0)
+
+    upper = lax.broadcasted_iota(jnp.int32, (8, LANES), 0) >= 4
 
     def unpack_p(c, carry):
-        col = pl.multiple_of(c * LANES, LANES)
         for b in range(blocks):
             lanes = slice(b * LANES, (b + 1) * LANES)
-            v = lane_swap(
-                [in_ref[per * b + i, :, pl.ds(col, LANES)].astype(F32) for i in range(per)]
-            )
             ctf = c_ref[pl.ds(pl.multiple_of(c * 2 * per, 2 * per), 2 * per), lanes]
-            for q in range(per):
-                row = pl.multiple_of((per * c + q) * 16, 16)
-                scale = jnp.concatenate(
-                    [
-                        jnp.broadcast_to(ctf[2 * q + odd : 2 * q + odd + 1], (8, LANES))
-                        for odd in range(2)
-                    ],
-                    axis=0,
+            for part in range(2):
+                col = pl.multiple_of((2 * c + part) * LANES, LANES)
+                v = lane_swap(
+                    [in_ref[per * b + i, :, pl.ds(col, LANES)].astype(F32) for i in range(per)]
                 )
-                p = v[q] * scale
-                cp_ref[pl.ds(row, 16), lanes] = p
-                swapped = flip_rows(p.reshape(2, 8, LANES)).reshape(16, LANES)
-                cq_ref[pl.ds(row, 16), lanes] = jnp.where(upper, swapped, -swapped)
+                for q in range(per):
+                    r = per * part + q
+                    row = pl.multiple_of((2 * per * c + r) * 8, 8)
+                    p = v[q] * jnp.broadcast_to(ctf[r : r + 1], (8, LANES))
+                    cp_ref[pl.ds(row, 8), lanes] = p
+                    swapped = flip_rows(p)
+                    cq_ref[pl.ds(row, 8), lanes] = jnp.where(upper, swapped, -swapped)
         return carry
 
-    lax.fori_loop(0, half // per, unpack_p, 0)
+    lax.fori_loop(0, cyc // (2 * per), unpack_p, 0)
 
     chunks, classes, wide = hot_ref.shape
     wide = wide // 8
     low = lax.broadcasted_iota(jnp.int32, (8, wide), 0) < 4
 
-    def chunk(t, carry):
-        col = pl.multiple_of(t * wide, wide)
-        cols = pl.ds(col, wide)
+    for t in range(chunks):
+        cols = slice(t * wide, (t + 1) * wide)
         for j in range(8):
             hot = one_hot(cid_s[j : j + 1, cols], classes)
             hot_ref[t, :, j * wide : (j + 1) * wide] = hot
@@ -221,9 +187,6 @@
             re = jnp.sum((cp_ref[:, cols] * picked).reshape(cyc, 8, wide), axis=0)
             im = jnp.sum((cq_ref[:, cols] * picked).reshape(cyc, 8, wide), axis=0)
             x_s[j, :, cols] = jnp.where(low, re + flip_rows(re), im + flip_rows(im))
-        return carry
-
-    lax.fori_loop(0, chunks, chunk, 0)
 
     for b in range(blocks):
         lanes = slice(b * LANES, (b + 1) * LANES)
@@ -309,7 +272,7 @@
                 out_ref[to, :, 4 * LANES :] = norm[k][0:2].astype(BF16)
 
 
-def finish_kernel(in_ref, order_ref, out_ref):
+def finish_kernel(in_ref, order_ref, out_ref, out_s):
     own, part, width = out_ref.shape
     every = in_ref.shape[0]
     src = width // 8
@@ -321,16 +284,19 @@
     for d in range(1, every // src):
         norm += in_ref[d * src, :, 4 * LANES :].astype(F32)
     x = jnp.concatenate([x, jnp.broadcast_to(norm[0:1], (8, LANES))], axis=0)
-    a = lax.broadcasted_iota(jnp.int32, (LANES, LANES), 0)
-    b = lax.broadcasted_iota(jnp.int32, (LANES, LANES), 1)
-    turn = jnp.where((a % own) * part + a // own == b, 1.0, 0.0)
-    x = jnp.dot(x, turn, precision=lax.Precision.HIGHEST, preferred_element_type=F32).T
-    out_ref[...] = (x[:, :width] / (x[:, width : width + 1] + 1.0)).reshape(own, part, width)
+    x = x.T
+    x = x[:, :width] / (x[:, width : width + 1] + 1.0)
+    for q in range(part):
+        for k in range(width // LANES):
+            lanes = slice(k * LANES, (k + 1) * LANES)
+            out_s[k, pl.ds(q, own, stride=part), :] = x[q * own : (q + 1) * own, lanes]
+    for k in range(width // LANES):
+        out_ref[:, :, k * LANES : (k + 1) * LANES] = out_s[k].reshape(own, part, LANES)
 
 
 def call(kernel, shapes, scratch, *args, space=pltpu.VMEM, limit=24):
     many = isinstance(shapes, (list, tuple)) and not hasattr(shapes, "dtype")
-    spec = pl.BlockSpec(memory_space=space)
+    spec = pl.BlockSpec(memory_space=pltpu.VMEM)
     return pl.pallas_call(
         kernel,
         out_shape=shapes,
@@ -360,30 +326,24 @@
     def exchange(x, axis):
         return lax.all_to_all(x, axis, split_axis=0, concat_axis=0, tiled=True)
 
-    width = (cyc // 2) * (n + own) + LANES
+    width = cyc * (n + own) + LANES
     sent = call(
         harmonics_kernel,
-        shape((owners, 16, width), BF16),
+        shape((owners, 8, width), BF16),
         [
             pltpu.VMEM((n, cyc, ang), BF16),
             pltpu.VMEM((own, cyc, ang), BF16),
             pltpu.VMEM((8, n), jnp.int32),
             pltpu.VMEM((1, n), jnp.int32),
             pltpu.VMEM((ang, ang), BF16),
-            pltpu.VMEM((owners, 16, width), BF16),
             pltpu.VMEM((ang // LANES, n * cyc, LANES), F32),
             pltpu.VMEM((ang // LANES, own * cyc, LANES), F32),
-            pltpu.VMEM((16, LANES), F32),
-            pltpu.SemaphoreType.DMA((11,)),
-            pltpu.SemaphoreType.DMA((9,)),
+            pltpu.VMEM((8, LANES), F32),
+            pltpu.SemaphoreType.DMA((5,)),
         ],
-        images,
-        references,
-        pri,
-        group,
-        jnp.asarray(forward, BF16),
+        *[pltpu.with_memory_space_constraint(x, pltpu.HBM) for x in (images, references, pri, group)],
+        pltpu.with_memory_space_constraint(jnp.asarray(forward, BF16), pltpu.HBM),
         space=pltpu.HBM,
-        limit=60,
     )
     got = exchange(sent, "cls")
     x, cp, cq, hot, ctf = call(
@@ -431,7 +391,7 @@
     return call(
         finish_kernel,
         shape((own, cyc // doms, ang), F32),
-        [],
+        [pltpu.VMEM((ang // LANES, own * cyc // doms, LANES), F32)],
         sums,
         jnp.asarray(pairs, BF16),
     )

time: 114 us -> 111 us (0.974)
  Pallas kernels: 24 us -> 22 us
    pallas_call x5, Pallas kernels: 24 us -> 22 us  [call(): pl.pallas_call(kernel, out_shape=shapes, in_specs=[pl.BlockSpec(memory_sp...]
where the time goes in v3:
time: 111 us
  blocking collectives  88.9 us (80%)
  Pallas kernels  22 us (20%)
    all_to_all x4, blocking collectives, exchange(): return lax.all_to_all(x, axis, split_axis=0, concat_axis=0, tiled=True)  88.9 us
    pallas_call x5, Pallas kernels, call(): pl.pallas_call(kernel, out_shape=shapes, in_specs=[pl.BlockSpec(memory_sp...  22 us

profile of v3, /device:TPU:1, one launch (start us, length us, event | category | flops | bytes accessed | tf_op | source)
XLA Modules:
  0.0 111.0 jit_solution(2623975448038458813)
XLA Ops:
  0.0 3.8 %shard_map.91 = bf16[32,8,3200]{2,1,0:T(8,128)(2,1)S(1)} custom-call(bf16[32,64,256]{2,1,0:T(8,128)(2,1)} %img_hbm.1, bf16[16,64,256]{2,1,0:T(8,128)(2,1)} %ref_hbm.1, s32[8,32]{1,0:T(8,128)} %bitcast.2, s32[1,32]{1,0:T(1,128)} %bitcast.3, bf16[256,256]{1,0:T(8,128)(2,1)} %constant.8.clone.fwd_hbm), custom_call_target="tpu_custom_call" | custom-call | tf_op jit(solution)/shard_map/pallas_call | solution.py:300
  3.8 0.0 copy-start.3
  3.8 0.0 copy-start.1
  3.9 0.0 copy-start.2
  3.9 32.0 %all_to_all.20.refs_0_ = bf16[32,8,3200]{2,1,0:T(8,128)(2,1)S(1)} all-to-all(bf16[32,8,3200]{2,1,0:T(8,128)(2,1)S(1)} %shard_map.91), channel_id=1, replica_groups=mesh['dom'=8,'cls'=32] {'cls'}, dimensions={0} | all-to-all | bytes 3276800 | tf_op jit(solution)/shard_map/all_to_all | solution.py:327
  35.9 0.0 copy-done.3
  35.9 9.1 %shard_map.92 = (f32[32,8,256]{2,1,0:T(8,128)S(1)}, f32[512,1024]{1,0:T(8,128)S(1)}, f32[512,1024]{1,0:T(8,128)S(1)}, bf16[4,512,2048]{2,1,0:T(8,128)(2,1)S(1)}, f32[64,1024]{1,0:T(8,128)S(1)}) custom-call(bf16[32,8,3200]{2,1,0:T(8,128)(2,1)S(1)} %all_to_all.20.refs_0_, f32[64,64]{1,0:T(8,128)S(1)} %copy-done.3), custom_call_target="tpu_custom_call" | custom-call | tf_op jit(solution)/shard_map/pallas_call | solution.py:300
  45.0 12.5 %all_to_all.21.x_ref = f32[32,8,256]{2,1,0:T(8,128)S(1)} all-to-all(f32[32,8,256]{2,1,0:T(8,128)S(1)} %get-tuple-element.10), channel_id=1, replica_groups=mesh['dom'=8,'cls'=32] {'cls'}, dimensions={0} | all-to-all | bytes 524288 | tf_op jit(solution)/shard_map/all_to_all | solution.py:327
  57.5 0.0 copy-done.1
  57.5 0.0 copy-done.2
  57.5 1.5 %shard_map.93 = bf16[32,8,256]{2,1,0:T(8,128)(2,1)S(1)} custom-call(f32[32,8,256]{2,1,0:T(8,128)S(1)} %all_to_all.21.x_ref, f32[256,256]{1,0:T(8,128)S(1)} %copy-done.2, f32[256,256]{1,0:T(8,128)S(1)} %copy-done.1), custom_call_target="tpu_custom_call" | custom-call | tf_op jit(solution)/shard_map/pallas_call | solution.py:300
  58.9 11.2 %all_to_all.22.w_ref = bf16[32,8,256]{2,1,0:T(8,128)(2,1)S(1)} all-to-all(bf16[32,8,256]{2,1,0:T(8,128)(2,1)S(1)} %shard_map.93), channel_id=1, replica_groups=mesh['dom'=8,'cls'=32] {'cls'}, dimensions={0} | all-to-all | bytes 262144 | tf_op jit(solution)/shard_map/all_to_all | solution.py:327
  70.1 0.0 copy-start
  70.1 6.3 %shard_map.94 = bf16[256,2,640]{2,1,0:T(2,128)(2,1)S(1)} custom-call(bf16[32,8,256]{2,1,0:T(8,128)(2,1)S(1)} %all_to_all.22.w_ref, f32[512,1024]{1,0:T(8,128)S(1)} %get-tuple-element.11.cp_ref, f32[512,1024]{1,0:T(8,128)S(1)} %get-tuple-element.12.cq_ref, bf16[4,512,2048]{2,1,0:T(8,128)(2,1)S(1)} %get-tuple-element.13.hot_ref, ...), custom_call_target="tpu_custom_call" | custom-call | tf_op jit(solution)/shard_map/pallas_call | solution.py:300
  76.4 33.3 %all_to_all.23.in_ref = bf16[256,2,640]{2,1,0:T(2,128)(2,1)S(1)} all-to-all(bf16[256,2,640]{2,1,0:T(2,128)(2,1)S(1)} %shard_map.94), channel_id=1, replica_groups=mesh['dom'=8,'cls'=32] {'dom','cls'}, dimensions={0} | all-to-all | bytes 1310720 | tf_op jit(solution)/shard_map/all_to_all | solution.py:327
  109.7 0.0 copy-done
  109.7 1.3 %shard_map.95 = f32[16,8,256]{2,1,0:T(8,128)} custom-call(bf16[256,2,640]{2,1,0:T(2,128)(2,1)S(1)} %all_to_all.23.in_ref, bf16[4,256,512]{2,1,0:T(8,128)(2,1)S(1)} %copy-done), custom_call_target="tpu_custom_call" | custom-call | tf_op jit(solution)/shard_map/pallas_call | solution.py:300
Async XLA Ops:
  3.8 32.1 %copy-start.3 = (f32[64,64]{1,0:T(8,128)S(1)}, f32[64,64]{1,0:T(8,128)}, u32[]{:S(2)}) copy-start(f32[64,64]{1,0:T(8,128)} %refs_1_.1) | copy-start | bytes 49156
  3.8 53.6 %copy-start.1 = (f32[256,256]{1,0:T(8,128)S(1)}, f32[256,256]{1,0:T(8,128)}, u32[]{:S(2)}) copy-start(f32[256,256]{1,0:T(8,128)} %constant.10.clone.fwd_ref) | copy-start | bytes 786436
  3.9 53.6 %copy-start.2 = (f32[256,256]{1,0:T(8,128)S(1)}, f32[256,256]{1,0:T(8,128)}, u32[]{:S(2)}) copy-start(f32[256,256]{1,0:T(8,128)} %constant.9.clone.inv_ref) | copy-start | bytes 786436
  70.1 39.6 %copy-start = (bf16[4,256,512]{2,1,0:T(8,128)(2,1)S(1)}, bf16[4,256,512]{2,1,0:T(8,128)(2,1)}, u32[]{:S(2)}) copy-start(bf16[4,256,512]{2,1,0:T(8,128)(2,1)} %constant.11.clone.order_ref) | copy-start | bytes 3145732

commit v4 on v3

--- a/solution.py
+++ b/solution.py
@@ -32,6 +32,14 @@
     return forward, inverse, order
 
 
+def swap_table(count):
+    size = count * LANES
+    to = np.arange(size).reshape(count, count, LANES // count).transpose(1, 0, 2).reshape(-1)
+    table = np.zeros((size, size), np.float32)
+    table[to, np.arange(size)] = 1.0
+    return jnp.asarray(table, BF16)
+
+
 def lane_swap(arrays):
     n = len(arrays)
     width = LANES // n
@@ -55,6 +63,8 @@
     n, cyc, ang = img_ref.shape
     own = ref_ref.shape[0]
     dest = out_ref.shape[0]
+    rows_p = 8 * cyc * n // LANES
+    rows_r = 8 * cyc * own // LANES
     pairs = (
         (fwd_hbm, fwd_ref),
         (ref_hbm, ref_ref),
@@ -66,7 +76,7 @@
     for copy in copies:
         copy.start()
 
-    def part(ref, src, count, column):
+    def part(ref, src, count, start):
         for k in range(ang // LANES):
             src[k] = ref[:, :, k * LANES : (k + 1) * LANES].astype(F32).reshape(count * cyc, LANES)
         wide = 2 * LANES
@@ -83,21 +93,21 @@
                 axis=1,
             ).astype(BF16)
             y = lax.dot_general(fwd_ref[...], block, NT, preferred_element_type=F32)
-            cut = slice(column + c * wide, column + (c + 1) * wide)
-            out_ref[:, :, cut] = y.reshape(dest, 8, wide).astype(BF16)
+            y = y.reshape(dest, 8, wide)
+            y = jnp.concatenate([y[:, :, :LANES], y[:, :, LANES:]], axis=1)
+            out_ref[:, start + 16 * c : start + 16 * (c + 1), :] = y.astype(BF16)
 
     copies[3].wait()
     copies[4].wait()
     int_s[...] = jnp.zeros_like(int_s)
     int_s[:, 0:n] = (pri_ref[...] - dest * own // 2).astype(F32)
     int_s[0:1, n : 2 * n] = def_ref[...].astype(F32)
-    column = cyc * (n + own)
-    out_ref[:, :, column : column + LANES] = jnp.broadcast_to(
+    out_ref[:, (rows_p + rows_r) :, :] = jnp.broadcast_to(
         int_s[...].astype(BF16)[None], (dest, 8, LANES)
     )
     copies[0].wait()
     copies[1].wait()
-    part(ref_ref, ref_s, own, cyc * n)
+    part(ref_ref, ref_s, own, rows_p)
     copies[2].wait()
     part(img_ref, img_s, n, 0)
 
@@ -114,13 +124,13 @@
     return pltpu.roll(x, 4, x.ndim - 2)
 
 
-def score_kernel(own, in_ref, ctf_ref, x_ref, cp_ref, cq_ref, hot_ref, c_ref, cid_s, rt_s, x_s):
+def score_kernel(own, in_ref, ctf_ref, swap_p_ref, swap_r_ref, x_ref, cp_ref, cq_ref, hot_ref, c_ref, cid_s, rt_s, x_s):
     src = in_ref.shape[0]
     groups, cyc = ctf_ref.shape
     total = cp_ref.shape[1]
     n = total // src
-    col_r = cyc * n
-    col_i = cyc * (n + own)
+    rows_p = 8 * cyc * n // LANES
+    rows_r = 8 * cyc * own // LANES
     per = LANES // n
     per_r = LANES // own
     blocks = src // per
@@ -129,7 +139,7 @@
     for b in range(blocks):
         lanes = slice(b * LANES, (b + 1) * LANES)
         v = lane_swap(
-            [in_ref[per * b + i, :, col_i : col_i + LANES].astype(F32) for i in range(per)]
+            [in_ref[per * b + i, (rows_p + rows_r) :, :].astype(F32) for i in range(per)]
         )
         cid_s[:, lanes] = v[0].astype(jnp.int32) + src * own // 2
         group = v[1][0:1].astype(jnp.int32)
@@ -138,41 +148,36 @@
             ctf_t, hot, precision=lax.Precision.HIGHEST, preferred_element_type=F32
         )
 
-    def unpack_r(c, carry):
-        col = pl.multiple_of(col_r + c * LANES, LANES)
-        for b in range(src // per_r):
-            v = lane_swap(
-                [in_ref[per_r * b + i, :, pl.ds(col, LANES)].astype(F32) for i in range(per_r)]
-            )
+    def swapped(first, last, size, table):
+        blocks = [
+            jnp.concatenate([in_ref[b + i, first:last, :] for i in range(size)], axis=1)
+            for b in range(0, src, size)
+        ]
+        return jnp.dot(jnp.concatenate(blocks, axis=0), table[...], preferred_element_type=F32)
+
+    every = swapped(rows_p, rows_p + rows_r, per_r, swap_r_ref).astype(BF16)
+    for b in range(src // per_r):
+        y = every[b * rows_r : (b + 1) * rows_r].reshape(rows_r // 8, 8, per_r * LANES)
+        for c in range(rows_r // 8):
             for q in range(0, per_r, 2):
-                row = pl.multiple_of((per_r * c + q) * 8, 16)
-                pair = jnp.concatenate([v[q], v[q + 1]], axis=0)
-                rt_s[pl.ds(row, 16), b * LANES : (b + 1) * LANES] = pair.astype(BF16)
-        return carry
-
-    lax.fori_loop(0, cyc // per_r, unpack_r, 0)
+                pair = [y[c, :, (q + k) * LANES : (q + k + 1) * LANES] for k in range(2)]
+                row = (per_r * c + q) * 8
+                rt_s[row : row + 16, b * LANES : (b + 1) * LANES] = jnp.concatenate(pair, axis=0)
 
     upper = lax.broadcasted_iota(jnp.int32, (8, LANES), 0) >= 4
-
-    def unpack_p(c, carry):
-        for b in range(blocks):
-            lanes = slice(b * LANES, (b + 1) * LANES)
-            ctf = c_ref[pl.ds(pl.multiple_of(c * 2 * per, 2 * per), 2 * per), lanes]
-            for part in range(2):
-                col = pl.multiple_of((2 * c + part) * LANES, LANES)
-                v = lane_swap(
-                    [in_ref[per * b + i, :, pl.ds(col, LANES)].astype(F32) for i in range(per)]
-                )
-                for q in range(per):
-                    r = per * part + q
-                    row = pl.multiple_of((2 * per * c + r) * 8, 8)
-                    p = v[q] * jnp.broadcast_to(ctf[r : r + 1], (8, LANES))
-                    cp_ref[pl.ds(row, 8), lanes] = p
-                    swapped = flip_rows(p)
-                    cq_ref[pl.ds(row, 8), lanes] = jnp.where(upper, swapped, -swapped)
-        return carry
-
-    lax.fori_loop(0, cyc // (2 * per), unpack_p, 0)
+    every = swapped(0, rows_p, per, swap_p_ref)
+    for b in range(blocks):
+        lanes = slice(b * LANES, (b + 1) * LANES)
+        y = every[b * rows_p : (b + 1) * rows_p]
+        ctf = c_ref[:, lanes]
+        for c in range(rows_p // 8):
+            for q in range(per):
+                r = per * c + q
+                p = y[8 * c : 8 * c + 8, q * LANES : (q + 1) * LANES]
+                p = p * jnp.broadcast_to(ctf[r : r + 1], (8, LANES))
+                cp_ref[8 * r : 8 * r + 8, lanes] = p
+                turned = flip_rows(p)
+                cq_ref[8 * r : 8 * r + 8, lanes] = jnp.where(upper, turned, -turned)
 
     chunks, classes, wide = hot_ref.shape
     wide = wide // 8
@@ -326,10 +331,10 @@
     def exchange(x, axis):
         return lax.all_to_all(x, axis, split_axis=0, concat_axis=0, tiled=True)
 
-    width = cyc * (n + own) + LANES
+    rows = 8 * (cyc * (n + own) // LANES + 1)
     sent = call(
         harmonics_kernel,
-        shape((owners, 8, width), BF16),
+        shape((owners, rows, LANES), BF16),
         [
             pltpu.VMEM((n, cyc, ang), BF16),
             pltpu.VMEM((own, cyc, ang), BF16),
@@ -362,6 +367,8 @@
         ],
         got,
         ctf_table,
+        swap_table(LANES // n),
+        swap_table(LANES // own),
     )
     x = exchange(x, "cls")
     spectrum = call(

time: 111 us -> 109 us (0.982)
  Pallas kernels: 22 us -> 19.7 us
    pallas_call x5, Pallas kernels: 22 us -> 19.7 us  [call(): pl.pallas_call(kernel, out_shape=shapes, in_specs=[pl.BlockSpec(memory_sp...]
where the time goes in v4:
time: 109 us
  blocking collectives  89 us (82%)
  Pallas kernels  19.7 us (18%)
    all_to_all x4, blocking collectives, exchange(): return lax.all_to_all(x, axis, split_axis=0, concat_axis=0, tiled=True)  89 us
    pallas_call x5, Pallas kernels, call(): pl.pallas_call(kernel, out_shape=shapes, in_specs=[pl.BlockSpec(memory_sp...  19.7 us

profile of v4, /device:TPU:1, one launch (start us, length us, event | category | flops | bytes accessed | tf_op | source)
XLA Modules:
  0.0 108.7 jit_solution(17709411823012434793)
XLA Ops:
  0.0 3.8 %shard_map.109 = bf16[32,200,128]{2,1,0:T(8,128)(2,1)S(1)} custom-call(bf16[32,64,256]{2,1,0:T(8,128)(2,1)} %img_hbm.1, bf16[16,64,256]{2,1,0:T(8,128)(2,1)} %ref_hbm.1, s32[8,32]{1,0:T(8,128)} %bitcast.2, s32[1,32]{1,0:T(1,128)} %bitcast.3, bf16[256,256]{1,0:T(8,128)(2,1)} %constant.12.clone.fwd_hbm), custom_call_target="tpu_custom_call" | custom-call | tf_op jit(solution)/shard_map/pallas_call | solution.py:305
  3.9 0.0 copy-start
  3.9 0.0 copy-start.2
  3.9 0.0 copy-start.5
  3.9 32.0 %all_to_all.20.refs_0_ = bf16[32,200,128]{2,1,0:T(8,128)(2,1)S(1)} all-to-all(bf16[32,200,128]{2,1,0:T(8,128)(2,1)S(1)} %shard_map.109), channel_id=1, replica_groups=mesh['dom'=8,'cls'=32] {'cls'}, dimensions={0} | all-to-all | bytes 3276800 | tf_op jit(solution)/shard_map/all_to_all | solution.py:332
  35.9 0.0 copy-done
  35.9 0.0 copy-done.2
  35.9 0.0 copy-done.5
  35.9 0.0 copy-start.3
  35.9 0.0 copy-start.4
  36.0 6.8 %shard_map.110 = (f32[32,8,256]{2,1,0:T(8,128)S(1)}, f32[512,1024]{1,0:T(8,128)S(1)}, f32[512,1024]{1,0:T(8,128)S(1)}, bf16[4,512,2048]{2,1,0:T(8,128)(2,1)S(1)}, f32[64,1024]{1,0:T(8,128)S(1)}) custom-call(bf16[32,200,128]{2,1,0:T(8,128)(2,1)S(1)} %all_to_all.20.refs_0_, f32[64,64]{1,0:T(8,128)S(1)} %copy-done.5, bf16[512,512]{1,0:T(8,128)(2,1)S(1)} %copy-done.2, ...), custom_call_target="tpu_custom_call" | custom-call | tf_op jit(solution)/shard_map/pallas_call | solution.py:305
  42.8 12.5 %all_to_all.21.x_ref = f32[32,8,256]{2,1,0:T(8,128)S(1)} all-to-all(f32[32,8,256]{2,1,0:T(8,128)S(1)} %get-tuple-element.10), channel_id=1, replica_groups=mesh['dom'=8,'cls'=32] {'cls'}, dimensions={0} | all-to-all | bytes 524288 | tf_op jit(solution)/shard_map/all_to_all | solution.py:332
  55.2 0.0 copy-done.3
  55.2 0.0 copy-done.4
  55.2 1.5 %shard_map.111 = bf16[32,8,256]{2,1,0:T(8,128)(2,1)S(1)} custom-call(f32[32,8,256]{2,1,0:T(8,128)S(1)} %all_to_all.21.x_ref, f32[256,256]{1,0:T(8,128)S(1)} %copy-done.4, f32[256,256]{1,0:T(8,128)S(1)} %copy-done.3), custom_call_target="tpu_custom_call" | custom-call | tf_op jit(solution)/shard_map/pallas_call | solution.py:305
  56.7 11.2 %all_to_all.22.w_ref = bf16[32,8,256]{2,1,0:T(8,128)(2,1)S(1)} all-to-all(bf16[32,8,256]{2,1,0:T(8,128)(2,1)S(1)} %shard_map.111), channel_id=1, replica_groups=mesh['dom'=8,'cls'=32] {'cls'}, dimensions={0} | all-to-all | bytes 262144 | tf_op jit(solution)/shard_map/all_to_all | solution.py:332
  67.9 0.0 copy-start.1
  67.9 6.3 %shard_map.112 = bf16[256,2,640]{2,1,0:T(2,128)(2,1)S(1)} custom-call(bf16[32,8,256]{2,1,0:T(8,128)(2,1)S(1)} %all_to_all.22.w_ref, f32[512,1024]{1,0:T(8,128)S(1)} %get-tuple-element.11.cp_ref, f32[512,1024]{1,0:T(8,128)S(1)} %get-tuple-element.12.cq_ref, bf16[4,512,2048]{2,1,0:T(8,128)(2,1)S(1)} %get-tuple-element.13.hot_ref, ...), custom_call_target="tpu_custom_call" | custom-call | tf_op jit(solution)/shard_map/pallas_call | solution.py:305
  74.2 33.3 %all_to_all.23.in_ref = bf16[256,2,640]{2,1,0:T(2,128)(2,1)S(1)} all-to-all(bf16[256,2,640]{2,1,0:T(2,128)(2,1)S(1)} %shard_map.112), channel_id=1, replica_groups=mesh['dom'=8,'cls'=32] {'dom','cls'}, dimensions={0} | all-to-all | bytes 1310720 | tf_op jit(solution)/shard_map/all_to_all | solution.py:332
  107.5 0.0 copy-done.1
  107.5 1.3 %shard_map.113 = f32[16,8,256]{2,1,0:T(8,128)} custom-call(bf16[256,2,640]{2,1,0:T(2,128)(2,1)S(1)} %all_to_all.23.in_ref, bf16[4,256,512]{2,1,0:T(8,128)(2,1)S(1)} %copy-done.1), custom_call_target="tpu_custom_call" | custom-call | tf_op jit(solution)/shard_map/pallas_call | solution.py:305
Async XLA Ops:
  3.9 32.1 %copy-start = (bf16[1024,1024]{1,0:T(8,128)(2,1)S(1)}, bf16[1024,1024]{1,0:T(8,128)(2,1)}, u32[]{:S(2)}) copy-start(bf16[1024,1024]{1,0:T(8,128)(2,1)} %constant.14.clone.refs_3_) | copy-start | bytes 6291460
  3.9 32.1 %copy-start.2 = (bf16[512,512]{1,0:T(8,128)(2,1)S(1)}, bf16[512,512]{1,0:T(8,128)(2,1)}, u32[]{:S(2)}) copy-start(bf16[512,512]{1,0:T(8,128)(2,1)} %constant.13.clone.refs_2_) | copy-start | bytes 1572868
  3.9 32.1 %copy-start.5 = (f32[64,64]{1,0:T(8,128)S(1)}, f32[64,64]{1,0:T(8,128)}, u32[]{:S(2)}) copy-start(f32[64,64]{1,0:T(8,128)} %refs_1_.1) | copy-start | bytes 49156
  35.9 19.3 %copy-start.3 = (f32[256,256]{1,0:T(8,128)S(1)}, f32[256,256]{1,0:T(8,128)}, u32[]{:S(2)}) copy-start(f32[256,256]{1,0:T(8,128)} %constant.16.clone.fwd_ref) | copy-start | bytes 786436
  35.9 19.3 %copy-start.4 = (f32[256,256]{1,0:T(8,128)S(1)}, f32[256,256]{1,0:T(8,128)}, u32[]{:S(2)}) copy-start(f32[256,256]{1,0:T(8,128)} %constant.15.clone.inv_ref) | copy-start | bytes 786436
  67.9 39.6 %copy-start.1 = (bf16[4,256,512]{2,1,0:T(8,128)(2,1)S(1)}, bf16[4,256,512]{2,1,0:T(8,128)(2,1)}, u32[]{:S(2)}) copy-start(bf16[4,256,512]{2,1,0:T(8,128)(2,1)} %constant.17.clone.order_ref) | copy-start | bytes 3145732

commit v5 on v4

--- a/solution.py
+++ b/solution.py
@@ -219,11 +219,13 @@
     part = jnp.broadcast_to(jnp.sum(grown, axis=0, keepdims=True), (8, slots))
     inverse = 1.0 / over_slots(part, jnp.add)
     weight = grown * inverse[0:1]
-    spectrum = jnp.dot(fwd_ref[...], weight, precision=high, preferred_element_type=F32)
+    spectrum = jnp.dot(
+        fwd_ref[...], weight, precision=lax.Precision.HIGH, preferred_element_type=F32
+    )
     out_ref[...] = spectrum.reshape(src, rows, slots).astype(out_ref.dtype)
 
 
-def sum_kernel(w_ref, cp_ref, cq_ref, hot_ref, c_ref, out_ref, w_s, t_s, sum_s):
+def sum_kernel(w_ref, cp_ref, cq_ref, hot_ref, c_ref, out_ref, w_s, t_s, sum_s, norm_s):
     src = w_ref.shape[0]
     feats, total = cp_ref.shape
     chunks, classes, wide = hot_ref.shape
@@ -241,40 +243,51 @@
                 w_s[per * u + j, :, lanes] = v[j]
 
     low = lax.broadcasted_iota(jnp.int32, (8, wide), 0) < 4
-    for t in range(chunks):
-        cols = slice(t * wide, (t + 1) * wide)
-        for j in range(8):
-            w = w_s[j, :, cols]
-            turned = flip_rows(w)
-            wc = jnp.where(low, w, turned)
-            ws = jnp.where(low, turned, w)
-            p = cp_ref[:, cols].reshape(cyc, 8, wide)
-            q = cq_ref[:, cols].reshape(cyc, 8, wide)
-            term = p * wc[None] - q * ws[None]
-            slot = slice(j * wide, (j + 1) * wide)
-            t_s[t % 2, 0:feats, slot] = term.reshape(feats, wide).astype(BF16)
-            c = c_ref[:, cols]
-            t_s[t % 2, feats:, slot] = (c * c * w[0:1]).astype(BF16)
-        part = lax.dot_general(t_s[t % 2], hot_ref[t], NT, preferred_element_type=F32)
-        if t == 0:
-            sum_s[...] = part
-        else:
-            sum_s[...] += part
     own = classes // src
     per = LANES // own
-    rows = 8 * per
-    for d in range(feats // rows):
+    doms = cyc // per
+    halves = sum_s.shape[0]
+    span = feats // halves
+    some = cyc // halves
+    for h in range(halves):
+        rows = slice(h * span, (h + 1) * span)
+        for t in range(chunks):
+            cols = slice(t * wide, (t + 1) * wide)
+            buf = t % 2
+            for j in range(8):
+                w = w_s[j, :, cols]
+                turned = flip_rows(w)
+                wc = jnp.where(low, w, turned)
+                ws = jnp.where(low, turned, w)
+                p = cp_ref[rows, cols].reshape(some, 8, wide)
+                q = cq_ref[rows, cols].reshape(some, 8, wide)
+                term = p * wc[None] - q * ws[None]
+                slot = slice(j * wide, (j + 1) * wide)
+                t_s[h, buf, 0:span, slot] = term.reshape(span, wide).astype(BF16)
+                c = c_ref[h * some : (h + 1) * some, cols]
+                t_s[h, buf, span:, slot] = (c * c * w[0:1]).astype(BF16)
+            part = lax.dot_general(t_s[h, buf], hot_ref[t], NT, preferred_element_type=F32)
+            if t == 0:
+                sum_s[h] = part
+            else:
+                sum_s[h] += part
+        norms = []
         for b in range(classes // LANES):
-            lanes = slice(b * LANES, (b + 1) * LANES)
-            v = lane_swap([sum_s[d * rows + 8 * q : d * rows + 8 * q + 8, lanes] for q in range(per)])
-            norm = sum_s[feats + d * per : feats + (d + 1) * per, lanes]
-            norm = lane_swap([jnp.broadcast_to(norm[q : q + 1], (8, LANES)) for q in range(per)])
-            for k in range(per):
-                part = v[k].astype(BF16)
-                to = d * src + per * b + k
-                for g in range(4):
-                    out_ref[to, :, g * LANES : (g + 1) * LANES] = part[2 * g : 2 * g + 2]
-                out_ref[to, :, 4 * LANES :] = norm[k][0:2].astype(BF16)
+            norm_s[h, b] = sum_s[h, span:, b * LANES : (b + 1) * LANES]
+            rows_q = [norm_s[h, b, pl.ds(q, doms // halves, stride=per), :] for q in range(per)]
+            norms.append(lane_swap(rows_q))
+        for d in range(doms // halves):
+            for b in range(classes // LANES):
+                lanes = slice(b * LANES, (b + 1) * LANES)
+                v = [sum_s[h, 8 * (d * per + q) : 8 * (d * per + q) + 8, lanes] for q in range(per)]
+                v = lane_swap(v)
+                for k in range(per):
+                    part = v[k].astype(BF16)
+                    to = (h * doms // halves + d) * src + per * b + k
+                    for g in range(4):
+                        out_ref[to, :, g * LANES : (g + 1) * LANES] = part[2 * g : 2 * g + 2]
+                    norm = jnp.broadcast_to(norms[b][k][d : d + 1], (2, LANES))
+                    out_ref[to, :, 4 * LANES :] = norm.astype(BF16)
 
 
 def finish_kernel(in_ref, order_ref, out_ref, out_s):
@@ -385,8 +398,9 @@
         shape((doms * owners, 2, 5 * LANES), BF16),
         [
             pltpu.VMEM((8, 8, total), F32),
-            pltpu.VMEM((2, feats + cyc, 8 * wide), BF16),
-            pltpu.VMEM((feats + cyc, classes), F32),
+            pltpu.VMEM((2, 2, (feats + cyc) // 2, 8 * wide), BF16),
+            pltpu.VMEM((2, (feats + cyc) // 2, classes), F32),
+            pltpu.VMEM((2, classes // LANES, cyc // 2, LANES), F32),
         ],
         spectrum,
         cp,

time: 109 us -> 108 us (level)
  no operation moved by 1% of the time
where the time goes in v5:
time: 108 us
  blocking collectives  89 us (82%)
  Pallas kernels  18.9 us (17%)
    all_to_all x4, blocking collectives, exchange(): return lax.all_to_all(x, axis, split_axis=0, concat_axis=0, tiled=True)  89 us
    pallas_call x5, Pallas kernels, call(): pl.pallas_call(kernel, out_shape=shapes, in_specs=[pl.BlockSpec(memory_sp...  18.9 us

profile of v5, /device:TPU:1, one launch (start us, length us, event | category | flops | bytes accessed | tf_op | source)
XLA Modules:
  0.0 108.0 jit_solution(13380721899804611532)
XLA Ops:
  0.0 3.8 %shard_map.109 = bf16[32,200,128]{2,1,0:T(8,128)(2,1)S(1)} custom-call(bf16[32,64,256]{2,1,0:T(8,128)(2,1)} %img_hbm.1, bf16[16,64,256]{2,1,0:T(8,128)(2,1)} %ref_hbm.1, s32[8,32]{1,0:T(8,128)} %bitcast.2, s32[1,32]{1,0:T(1,128)} %bitcast.3, bf16[256,256]{1,0:T(8,128)(2,1)} %constant.12.clone.fwd_hbm), custom_call_target="tpu_custom_call" | custom-call | tf_op jit(solution)/shard_map/pallas_call | solution.py:318
  3.9 0.0 copy-start
  3.9 0.0 copy-start.2
  3.9 0.0 copy-start.5
  3.9 32.0 %all_to_all.20.refs_0_ = bf16[32,200,128]{2,1,0:T(8,128)(2,1)S(1)} all-to-all(bf16[32,200,128]{2,1,0:T(8,128)(2,1)S(1)} %shard_map.109), channel_id=1, replica_groups=mesh['dom'=8,'cls'=32] {'cls'}, dimensions={0} | all-to-all | bytes 3276800 | tf_op jit(solution)/shard_map/all_to_all | solution.py:345
  35.9 0.0 copy-done
  35.9 0.0 copy-done.2
  35.9 0.0 copy-done.5
  35.9 0.0 copy-start.3
  35.9 0.0 copy-start.4
  36.0 6.8 %shard_map.110 = (f32[32,8,256]{2,1,0:T(8,128)S(1)}, f32[512,1024]{1,0:T(8,128)S(1)}, f32[512,1024]{1,0:T(8,128)S(1)}, bf16[4,512,2048]{2,1,0:T(8,128)(2,1)S(1)}, f32[64,1024]{1,0:T(8,128)S(1)}) custom-call(bf16[32,200,128]{2,1,0:T(8,128)(2,1)S(1)} %all_to_all.20.refs_0_, f32[64,64]{1,0:T(8,128)S(1)} %copy-done.5, bf16[512,512]{1,0:T(8,128)(2,1)S(1)} %copy-done.2, ...), custom_call_target="tpu_custom_call" | custom-call | tf_op jit(solution)/shard_map/pallas_call | solution.py:318
  42.8 12.5 %all_to_all.21.x_ref = f32[32,8,256]{2,1,0:T(8,128)S(1)} all-to-all(f32[32,8,256]{2,1,0:T(8,128)S(1)} %get-tuple-element.10), channel_id=1, replica_groups=mesh['dom'=8,'cls'=32] {'cls'}, dimensions={0} | all-to-all | bytes 524288 | tf_op jit(solution)/shard_map/all_to_all | solution.py:345
  55.2 0.0 copy-done.3
  55.2 0.0 copy-done.4
  55.2 1.2 %shard_map.111 = bf16[32,8,256]{2,1,0:T(8,128)(2,1)S(1)} custom-call(f32[32,8,256]{2,1,0:T(8,128)S(1)} %all_to_all.21.x_ref, f32[256,256]{1,0:T(8,128)S(1)} %copy-done.4, f32[256,256]{1,0:T(8,128)S(1)} %copy-done.3), custom_call_target="tpu_custom_call" | custom-call | tf_op jit(solution)/shard_map/pallas_call | solution.py:318
  56.4 11.2 %all_to_all.22.w_ref = bf16[32,8,256]{2,1,0:T(8,128)(2,1)S(1)} all-to-all(bf16[32,8,256]{2,1,0:T(8,128)(2,1)S(1)} %shard_map.111), channel_id=1, replica_groups=mesh['dom'=8,'cls'=32] {'cls'}, dimensions={0} | all-to-all | bytes 262144 | tf_op jit(solution)/shard_map/all_to_all | solution.py:345
  67.6 0.0 copy-start.1
  67.6 5.9 %shard_map.112 = bf16[256,2,640]{2,1,0:T(2,128)(2,1)S(1)} custom-call(bf16[32,8,256]{2,1,0:T(8,128)(2,1)S(1)} %all_to_all.22.w_ref, f32[512,1024]{1,0:T(8,128)S(1)} %get-tuple-element.11.cp_ref, f32[512,1024]{1,0:T(8,128)S(1)} %get-tuple-element.12.cq_ref, bf16[4,512,2048]{2,1,0:T(8,128)(2,1)S(1)} %get-tuple-element.13.hot_ref, ...), custom_call_target="tpu_custom_call" | custom-call | tf_op jit(solution)/shard_map/pallas_call | solution.py:318
  73.4 33.3 %all_to_all.23.in_ref = bf16[256,2,640]{2,1,0:T(2,128)(2,1)S(1)} all-to-all(bf16[256,2,640]{2,1,0:T(2,128)(2,1)S(1)} %shard_map.112), channel_id=1, replica_groups=mesh['dom'=8,'cls'=32] {'dom','cls'}, dimensions={0} | all-to-all | bytes 1310720 | tf_op jit(solution)/shard_map/all_to_all | solution.py:345
  106.7 0.0 copy-done.1
  106.7 1.3 %shard_map.113 = f32[16,8,256]{2,1,0:T(8,128)} custom-call(bf16[256,2,640]{2,1,0:T(2,128)(2,1)S(1)} %all_to_all.23.in_ref, bf16[4,256,512]{2,1,0:T(8,128)(2,1)S(1)} %copy-done.1), custom_call_target="tpu_custom_call" | custom-call | tf_op jit(solution)/shard_map/pallas_call | solution.py:318
Async XLA Ops:
  3.9 32.1 %copy-start = (bf16[1024,1024]{1,0:T(8,128)(2,1)S(1)}, bf16[1024,1024]{1,0:T(8,128)(2,1)}, u32[]{:S(2)}) copy-start(bf16[1024,1024]{1,0:T(8,128)(2,1)} %constant.14.clone.refs_3_) | copy-start | bytes 6291460
  3.9 32.1 %copy-start.2 = (bf16[512,512]{1,0:T(8,128)(2,1)S(1)}, bf16[512,512]{1,0:T(8,128)(2,1)}, u32[]{:S(2)}) copy-start(bf16[512,512]{1,0:T(8,128)(2,1)} %constant.13.clone.refs_2_) | copy-start | bytes 1572868
  3.9 32.1 %copy-start.5 = (f32[64,64]{1,0:T(8,128)S(1)}, f32[64,64]{1,0:T(8,128)}, u32[]{:S(2)}) copy-start(f32[64,64]{1,0:T(8,128)} %refs_1_.1) | copy-start | bytes 49156
  35.9 19.3 %copy-start.3 = (f32[256,256]{1,0:T(8,128)S(1)}, f32[256,256]{1,0:T(8,128)}, u32[]{:S(2)}) copy-start(f32[256,256]{1,0:T(8,128)} %constant.16.clone.fwd_ref) | copy-start | bytes 786436
  35.9 19.3 %copy-start.4 = (f32[256,256]{1,0:T(8,128)S(1)}, f32[256,256]{1,0:T(8,128)}, u32[]{:S(2)}) copy-start(f32[256,256]{1,0:T(8,128)} %constant.15.clone.inv_ref) | copy-start | bytes 786436
  67.6 39.2 %copy-start.1 = (bf16[4,256,512]{2,1,0:T(8,128)(2,1)S(1)}, bf16[4,256,512]{2,1,0:T(8,128)(2,1)}, u32[]{:S(2)}) copy-start(bf16[4,256,512]{2,1,0:T(8,128)(2,1)} %constant.17.clone.order_ref) | copy-start | bytes 3145732

commit v6 on v5

--- a/solution.py
+++ b/solution.py
@@ -135,7 +135,13 @@
     per_r = LANES // own
     blocks = src // per
 
-    ctf_t = ctf_ref[...].T
+    ctf = ctf_ref[...]
+    parts = []
+    for _ in range(3):
+        parts.append(ctf.astype(BF16).astype(F32))
+        ctf = ctf - parts[-1]
+    parts = jnp.concatenate(parts, axis=0).T.astype(BF16)
+    hots = []
     for b in range(blocks):
         lanes = slice(b * LANES, (b + 1) * LANES)
         v = lane_swap(
@@ -143,19 +149,19 @@
         )
         cid_s[:, lanes] = v[0].astype(jnp.int32) + src * own // 2
         group = v[1][0:1].astype(jnp.int32)
-        hot = (lax.broadcasted_iota(jnp.int32, (groups, LANES), 0) == group).astype(F32)
-        c_ref[:, lanes] = jnp.dot(
-            ctf_t, hot, precision=lax.Precision.HIGHEST, preferred_element_type=F32
-        )
-
-    def swapped(first, last, size, table):
+        hots.append((lax.broadcasted_iota(jnp.int32, (groups, LANES), 0) == group).astype(F32))
+    hots = jnp.concatenate(hots, axis=1)
+    hots = jnp.concatenate([hots] * 3, axis=0).astype(BF16)
+    c_ref[...] = jnp.dot(parts, hots, preferred_element_type=F32)
+
+    def swapped(sources, first, last, size, table):
         blocks = [
             jnp.concatenate([in_ref[b + i, first:last, :] for i in range(size)], axis=1)
-            for b in range(0, src, size)
+            for b in range(sources.start, sources.stop, size)
         ]
         return jnp.dot(jnp.concatenate(blocks, axis=0), table[...], preferred_element_type=F32)
 
-    every = swapped(rows_p, rows_p + rows_r, per_r, swap_r_ref).astype(BF16)
+    every = swapped(range(src), rows_p, rows_p + rows_r, per_r, swap_r_ref).astype(BF16)
     for b in range(src // per_r):
         y = every[b * rows_r : (b + 1) * rows_r].reshape(rows_r // 8, 8, per_r * LANES)
         for c in range(rows_r // 8):
@@ -165,10 +171,9 @@
                 rt_s[row : row + 16, b * LANES : (b + 1) * LANES] = jnp.concatenate(pair, axis=0)
 
     upper = lax.broadcasted_iota(jnp.int32, (8, LANES), 0) >= 4
-    every = swapped(0, rows_p, per, swap_p_ref)
-    for b in range(blocks):
+
+    def scale(b, y):
         lanes = slice(b * LANES, (b + 1) * LANES)
-        y = every[b * rows_p : (b + 1) * rows_p]
         ctf = c_ref[:, lanes]
         for c in range(rows_p // 8):
             for q in range(per):
@@ -185,6 +190,12 @@
 
     for t in range(chunks):
         cols = slice(t * wide, (t + 1) * wide)
+        if t % 2 == 0:
+            sources = range(t * wide // n, (t + 2) * wide // n)
+            every = swapped(sources, 0, rows_p, per, swap_p_ref)
+        for b in range(wide // LANES):
+            at = (t % 2 * wide // LANES + b) * rows_p
+            scale(t * wide // LANES + b, every[at : at + rows_p])
         for j in range(8):
             hot = one_hot(cid_s[j : j + 1, cols], classes)
             hot_ref[t, :, j * wide : (j + 1) * wide] = hot

time: 108 us -> 108 us (level)
  no operation moved by 1% of the time
where the time goes in v6:
time: 108 us
  blocking collectives  88.9 us (82%)
  Pallas kernels  18.7 us (17%)
    all_to_all x4, blocking collectives, exchange(): return lax.all_to_all(x, axis, split_axis=0, concat_axis=0, tiled=True)  88.9 us
    pallas_call x5, Pallas kernels, call(): pl.pallas_call(kernel, out_shape=shapes, in_specs=[pl.BlockSpec(memory_sp...  18.7 us

profile of v6, /device:TPU:1, one launch (start us, length us, event | category | flops | bytes accessed | tf_op | source)
XLA Modules:
  0.0 107.7 jit_solution(2839371412558017395)
XLA Ops:
  0.0 3.8 %shard_map.109 = bf16[32,200,128]{2,1,0:T(8,128)(2,1)S(1)} custom-call(bf16[32,64,256]{2,1,0:T(8,128)(2,1)} %img_hbm.1, bf16[16,64,256]{2,1,0:T(8,128)(2,1)} %ref_hbm.1, s32[8,32]{1,0:T(8,128)} %bitcast.2, s32[1,32]{1,0:T(1,128)} %bitcast.3, bf16[256,256]{1,0:T(8,128)(2,1)} %constant.12.clone.fwd_hbm), custom_call_target="tpu_custom_call" | custom-call | tf_op jit(solution)/shard_map/pallas_call | solution.py:329
  3.9 0.0 copy-start
  3.9 0.0 copy-start.2
  3.9 0.0 copy-start.5
  3.9 32.0 %all_to_all.20.refs_0_ = bf16[32,200,128]{2,1,0:T(8,128)(2,1)S(1)} all-to-all(bf16[32,200,128]{2,1,0:T(8,128)(2,1)S(1)} %shard_map.109), channel_id=1, replica_groups=mesh['dom'=8,'cls'=32] {'cls'}, dimensions={0} | all-to-all | bytes 3276800 | tf_op jit(solution)/shard_map/all_to_all | solution.py:356
  35.9 0.0 copy-done
  35.9 0.0 copy-done.2
  35.9 0.0 copy-done.5
  35.9 0.0 copy-start.3
  35.9 0.0 copy-start.4
  36.0 6.5 %shard_map.110 = (f32[32,8,256]{2,1,0:T(8,128)S(1)}, f32[512,1024]{1,0:T(8,128)S(1)}, f32[512,1024]{1,0:T(8,128)S(1)}, bf16[4,512,2048]{2,1,0:T(8,128)(2,1)S(1)}, f32[64,1024]{1,0:T(8,128)S(1)}) custom-call(bf16[32,200,128]{2,1,0:T(8,128)(2,1)S(1)} %all_to_all.20.refs_0_, f32[64,64]{1,0:T(8,128)S(1)} %copy-done.5, bf16[512,512]{1,0:T(8,128)(2,1)S(1)} %copy-done.2, ...), custom_call_target="tpu_custom_call" | custom-call | tf_op jit(solution)/shard_map/pallas_call | solution.py:329
  42.5 12.5 %all_to_all.21.x_ref = f32[32,8,256]{2,1,0:T(8,128)S(1)} all-to-all(f32[32,8,256]{2,1,0:T(8,128)S(1)} %get-tuple-element.10), channel_id=1, replica_groups=mesh['dom'=8,'cls'=32] {'cls'}, dimensions={0} | all-to-all | bytes 524288 | tf_op jit(solution)/shard_map/all_to_all | solution.py:356
  55.0 0.0 copy-done.3
  55.0 0.0 copy-done.4
  55.0 1.2 %shard_map.111 = bf16[32,8,256]{2,1,0:T(8,128)(2,1)S(1)} custom-call(f32[32,8,256]{2,1,0:T(8,128)S(1)} %all_to_all.21.x_ref, f32[256,256]{1,0:T(8,128)S(1)} %copy-done.4, f32[256,256]{1,0:T(8,128)S(1)} %copy-done.3), custom_call_target="tpu_custom_call" | custom-call | tf_op jit(solution)/shard_map/pallas_call | solution.py:329
  56.1 11.2 %all_to_all.22.w_ref = bf16[32,8,256]{2,1,0:T(8,128)(2,1)S(1)} all-to-all(bf16[32,8,256]{2,1,0:T(8,128)(2,1)S(1)} %shard_map.111), channel_id=1, replica_groups=mesh['dom'=8,'cls'=32] {'cls'}, dimensions={0} | all-to-all | bytes 262144 | tf_op jit(solution)/shard_map/all_to_all | solution.py:356
  67.3 0.0 copy-start.1
  67.3 5.9 %shard_map.112 = bf16[256,2,640]{2,1,0:T(2,128)(2,1)S(1)} custom-call(bf16[32,8,256]{2,1,0:T(8,128)(2,1)S(1)} %all_to_all.22.w_ref, f32[512,1024]{1,0:T(8,128)S(1)} %get-tuple-element.11.cp_ref, f32[512,1024]{1,0:T(8,128)S(1)} %get-tuple-element.12.cq_ref, bf16[4,512,2048]{2,1,0:T(8,128)(2,1)S(1)} %get-tuple-element.13.hot_ref, ...), custom_call_target="tpu_custom_call" | custom-call | tf_op jit(solution)/shard_map/pallas_call | solution.py:329
  73.2 33.3 %all_to_all.23.in_ref = bf16[256,2,640]{2,1,0:T(2,128)(2,1)S(1)} all-to-all(bf16[256,2,640]{2,1,0:T(2,128)(2,1)S(1)} %shard_map.112), channel_id=1, replica_groups=mesh['dom'=8,'cls'=32] {'dom','cls'}, dimensions={0} | all-to-all | bytes 1310720 | tf_op jit(solution)/shard_map/all_to_all | solution.py:356
  106.5 0.0 copy-done.1
  106.5 1.3 %shard_map.113 = f32[16,8,256]{2,1,0:T(8,128)} custom-call(bf16[256,2,640]{2,1,0:T(2,128)(2,1)S(1)} %all_to_all.23.in_ref, bf16[4,256,512]{2,1,0:T(8,128)(2,1)S(1)} %copy-done.1), custom_call_target="tpu_custom_call" | custom-call | tf_op jit(solution)/shard_map/pallas_call | solution.py:329
Async XLA Ops:
  3.9 32.1 %copy-start = (bf16[1024,1024]{1,0:T(8,128)(2,1)S(1)}, bf16[1024,1024]{1,0:T(8,128)(2,1)}, u32[]{:S(2)}) copy-start(bf16[1024,1024]{1,0:T(8,128)(2,1)} %constant.14.clone.refs_3_) | copy-start | bytes 6291460
  3.9 32.1 %copy-start.2 = (bf16[512,512]{1,0:T(8,128)(2,1)S(1)}, bf16[512,512]{1,0:T(8,128)(2,1)}, u32[]{:S(2)}) copy-start(bf16[512,512]{1,0:T(8,128)(2,1)} %constant.13.clone.refs_2_) | copy-start | bytes 1572868
  3.9 32.1 %copy-start.5 = (f32[64,64]{1,0:T(8,128)S(1)}, f32[64,64]{1,0:T(8,128)}, u32[]{:S(2)}) copy-start(f32[64,64]{1,0:T(8,128)} %refs_1_.1) | copy-start | bytes 49156
  35.9 19.0 %copy-start.3 = (f32[256,256]{1,0:T(8,128)S(1)}, f32[256,256]{1,0:T(8,128)}, u32[]{:S(2)}) copy-start(f32[256,256]{1,0:T(8,128)} %constant.16.clone.fwd_ref) | copy-start | bytes 786436
  35.9 19.0 %copy-start.4 = (f32[256,256]{1,0:T(8,128)S(1)}, f32[256,256]{1,0:T(8,128)}, u32[]{:S(2)}) copy-start(f32[256,256]{1,0:T(8,128)} %constant.15.clone.inv_ref) | copy-start | bytes 786436
  67.3 39.2 %copy-start.1 = (bf16[4,256,512]{2,1,0:T(8,128)(2,1)S(1)}, bf16[4,256,512]{2,1,0:T(8,128)(2,1)}, u32[]{:S(2)}) copy-start(bf16[4,256,512]{2,1,0:T(8,128)(2,1)} %constant.17.clone.order_ref) | copy-start | bytes 3145732

commit v7 on v6

--- a/solution.py
+++ b/solution.py
@@ -97,6 +97,11 @@
             y = jnp.concatenate([y[:, :, :LANES], y[:, :, LANES:]], axis=1)
             out_ref[:, start + 16 * c : start + 16 * (c + 1), :] = y.astype(BF16)
 
+    copies[0].wait()
+    copies[1].wait()
+    part(ref_ref, ref_s, own, rows_p)
+    copies[2].wait()
+    part(img_ref, img_s, n, 0)
     copies[3].wait()
     copies[4].wait()
     int_s[...] = jnp.zeros_like(int_s)
@@ -105,11 +110,6 @@
     out_ref[:, (rows_p + rows_r) :, :] = jnp.broadcast_to(
         int_s[...].astype(BF16)[None], (dest, 8, LANES)
     )
-    copies[0].wait()
-    copies[1].wait()
-    part(ref_ref, ref_s, own, rows_p)
-    copies[2].wait()
-    part(img_ref, img_s, n, 0)
 
 
 def one_hot(row, count):

time: 108 us -> 108 us (level)
  no operation moved by 1% of the time
where the time goes in v7:
time: 108 us
  blocking collectives  88.9 us (82%)
  Pallas kernels  18.6 us (17%)
    all_to_all x4, blocking collectives, exchange(): return lax.all_to_all(x, axis, split_axis=0, concat_axis=0, tiled=True)  88.9 us
    pallas_call x5, Pallas kernels, call(): pl.pallas_call(kernel, out_shape=shapes, in_specs=[pl.BlockSpec(memory_sp...  18.6 us

profile of v7, /device:TPU:1, one launch (start us, length us, event | category | flops | bytes accessed | tf_op | source)
XLA Modules:
  0.0 107.6 jit_solution(12202418809248104410)
XLA Ops:
  0.0 3.7 %shard_map.109 = bf16[32,200,128]{2,1,0:T(8,128)(2,1)S(1)} custom-call(bf16[32,64,256]{2,1,0:T(8,128)(2,1)} %img_hbm.1, bf16[16,64,256]{2,1,0:T(8,128)(2,1)} %ref_hbm.1, s32[8,32]{1,0:T(8,128)} %bitcast.2, s32[1,32]{1,0:T(1,128)} %bitcast.3, bf16[256,256]{1,0:T(8,128)(2,1)} %constant.12.clone.fwd_hbm), custom_call_target="tpu_custom_call" | custom-call | tf_op jit(solution)/shard_map/pallas_call | solution.py:329
  3.7 0.0 copy-start
  3.8 0.0 copy-start.2
  3.8 0.0 copy-start.5
  3.8 32.0 %all_to_all.20.refs_0_ = bf16[32,200,128]{2,1,0:T(8,128)(2,1)S(1)} all-to-all(bf16[32,200,128]{2,1,0:T(8,128)(2,1)S(1)} %shard_map.109), channel_id=1, replica_groups=mesh['dom'=8,'cls'=32] {'cls'}, dimensions={0} | all-to-all | bytes 3276800 | tf_op jit(solution)/shard_map/all_to_all | solution.py:356
  35.8 0.0 copy-done
  35.8 0.0 copy-done.2
  35.8 0.0 copy-done.5
  35.8 0.0 copy-start.3
  35.8 0.0 copy-start.4
  35.9 6.5 %shard_map.110 = (f32[32,8,256]{2,1,0:T(8,128)S(1)}, f32[512,1024]{1,0:T(8,128)S(1)}, f32[512,1024]{1,0:T(8,128)S(1)}, bf16[4,512,2048]{2,1,0:T(8,128)(2,1)S(1)}, f32[64,1024]{1,0:T(8,128)S(1)}) custom-call(bf16[32,200,128]{2,1,0:T(8,128)(2,1)S(1)} %all_to_all.20.refs_0_, f32[64,64]{1,0:T(8,128)S(1)} %copy-done.5, bf16[512,512]{1,0:T(8,128)(2,1)S(1)} %copy-done.2, ...), custom_call_target="tpu_custom_call" | custom-call | tf_op jit(solution)/shard_map/pallas_call | solution.py:329
  42.4 12.5 %all_to_all.21.x_ref = f32[32,8,256]{2,1,0:T(8,128)S(1)} all-to-all(f32[32,8,256]{2,1,0:T(8,128)S(1)} %get-tuple-element.10), channel_id=1, replica_groups=mesh['dom'=8,'cls'=32] {'cls'}, dimensions={0} | all-to-all | bytes 524288 | tf_op jit(solution)/shard_map/all_to_all | solution.py:356
  54.8 0.0 copy-done.3
  54.8 0.0 copy-done.4
  54.8 1.2 %shard_map.111 = bf16[32,8,256]{2,1,0:T(8,128)(2,1)S(1)} custom-call(f32[32,8,256]{2,1,0:T(8,128)S(1)} %all_to_all.21.x_ref, f32[256,256]{1,0:T(8,128)S(1)} %copy-done.4, f32[256,256]{1,0:T(8,128)S(1)} %copy-done.3), custom_call_target="tpu_custom_call" | custom-call | tf_op jit(solution)/shard_map/pallas_call | solution.py:329
  56.0 11.2 %all_to_all.22.w_ref = bf16[32,8,256]{2,1,0:T(8,128)(2,1)S(1)} all-to-all(bf16[32,8,256]{2,1,0:T(8,128)(2,1)S(1)} %shard_map.111), channel_id=1, replica_groups=mesh['dom'=8,'cls'=32] {'cls'}, dimensions={0} | all-to-all | bytes 262144 | tf_op jit(solution)/shard_map/all_to_all | solution.py:356
  67.2 0.0 copy-start.1
  67.2 5.9 %shard_map.112 = bf16[256,2,640]{2,1,0:T(2,128)(2,1)S(1)} custom-call(bf16[32,8,256]{2,1,0:T(8,128)(2,1)S(1)} %all_to_all.22.w_ref, f32[512,1024]{1,0:T(8,128)S(1)} %get-tuple-element.11.cp_ref, f32[512,1024]{1,0:T(8,128)S(1)} %get-tuple-element.12.cq_ref, bf16[4,512,2048]{2,1,0:T(8,128)(2,1)S(1)} %get-tuple-element.13.hot_ref, ...), custom_call_target="tpu_custom_call" | custom-call | tf_op jit(solution)/shard_map/pallas_call | solution.py:329
  73.1 33.3 %all_to_all.23.in_ref = bf16[256,2,640]{2,1,0:T(2,128)(2,1)S(1)} all-to-all(bf16[256,2,640]{2,1,0:T(2,128)(2,1)S(1)} %shard_map.112), channel_id=1, replica_groups=mesh['dom'=8,'cls'=32] {'dom','cls'}, dimensions={0} | all-to-all | bytes 1310720 | tf_op jit(solution)/shard_map/all_to_all | solution.py:356
  106.4 0.0 copy-done.1
  106.4 1.3 %shard_map.113 = f32[16,8,256]{2,1,0:T(8,128)} custom-call(bf16[256,2,640]{2,1,0:T(2,128)(2,1)S(1)} %all_to_all.23.in_ref, bf16[4,256,512]{2,1,0:T(8,128)(2,1)S(1)} %copy-done.1), custom_call_target="tpu_custom_call" | custom-call | tf_op jit(solution)/shard_map/pallas_call | solution.py:329
Async XLA Ops:
  3.7 32.1 %copy-start = (bf16[1024,1024]{1,0:T(8,128)(2,1)S(1)}, bf16[1024,1024]{1,0:T(8,128)(2,1)}, u32[]{:S(2)}) copy-start(bf16[1024,1024]{1,0:T(8,128)(2,1)} %constant.14.clone.refs_3_) | copy-start | bytes 6291460
  3.8 32.1 %copy-start.2 = (bf16[512,512]{1,0:T(8,128)(2,1)S(1)}, bf16[512,512]{1,0:T(8,128)(2,1)}, u32[]{:S(2)}) copy-start(bf16[512,512]{1,0:T(8,128)(2,1)} %constant.13.clone.refs_2_) | copy-start | bytes 1572868
  3.8 32.1 %copy-start.5 = (f32[64,64]{1,0:T(8,128)S(1)}, f32[64,64]{1,0:T(8,128)}, u32[]{:S(2)}) copy-start(f32[64,64]{1,0:T(8,128)} %refs_1_.1) | copy-start | bytes 49156
  35.8 19.0 %copy-start.3 = (f32[256,256]{1,0:T(8,128)S(1)}, f32[256,256]{1,0:T(8,128)}, u32[]{:S(2)}) copy-start(f32[256,256]{1,0:T(8,128)} %constant.16.clone.fwd_ref) | copy-start | bytes 786436
  35.8 19.0 %copy-start.4 = (f32[256,256]{1,0:T(8,128)S(1)}, f32[256,256]{1,0:T(8,128)}, u32[]{:S(2)}) copy-start(f32[256,256]{1,0:T(8,128)} %constant.15.clone.inv_ref) | copy-start | bytes 786436
  67.2 39.2 %copy-start.1 = (bf16[4,256,512]{2,1,0:T(8,128)(2,1)S(1)}, bf16[4,256,512]{2,1,0:T(8,128)(2,1)}, u32[]{:S(2)}) copy-start(bf16[4,256,512]{2,1,0:T(8,128)(2,1)} %constant.17.clone.order_ref) | copy-start | bytes 3145732

commit v8 on v7

--- a/solution.py
+++ b/solution.py
@@ -68,9 +68,10 @@
     pairs = (
         (fwd_hbm, fwd_ref),
         (ref_hbm, ref_ref),
-        (img_hbm, img_ref),
+        (img_hbm.at[0 : n // 2], img_ref.at[0 : n // 2]),
         (pri_hbm, pri_ref),
         (def_hbm, def_ref),
+        (img_hbm.at[n // 2 : n], img_ref.at[n // 2 : n]),
     )
     copies = [pltpu.make_async_copy(a, b, sems.at[k]) for k, (a, b) in enumerate(pairs)]
     for copy in copies:
@@ -101,6 +102,7 @@
     copies[1].wait()
     part(ref_ref, ref_s, own, rows_p)
     copies[2].wait()
+    copies[5].wait()
     part(img_ref, img_s, n, 0)
     copies[3].wait()
     copies[4].wait()
@@ -368,7 +370,7 @@
             pltpu.VMEM((ang // LANES, n * cyc, LANES), F32),
             pltpu.VMEM((ang // LANES, own * cyc, LANES), F32),
             pltpu.VMEM((8, LANES), F32),
-            pltpu.SemaphoreType.DMA((5,)),
+            pltpu.SemaphoreType.DMA((6,)),
         ],
         *[pltpu.with_memory_space_constraint(x, pltpu.HBM) for x in (images, references, pri, group)],
         pltpu.with_memory_space_constraint(jnp.asarray(forward, BF16), pltpu.HBM),

time: 108 us -> 108 us (level)
  no operation moved by 1% of the time
where the time goes in v8:
time: 108 us
  blocking collectives  88.9 us (82%)
  Pallas kernels  18.6 us (17%)
    all_to_all x4, blocking collectives, exchange(): return lax.all_to_all(x, axis, split_axis=0, concat_axis=0, tiled=True)  88.9 us
    pallas_call x5, Pallas kernels, call(): pl.pallas_call(kernel, out_shape=shapes, in_specs=[pl.BlockSpec(memory_sp...  18.6 us

profile of v8, /device:TPU:1, one launch (start us, length us, event | category | flops | bytes accessed | tf_op | source)
XLA Modules:
  0.0 107.6 jit_solution(7682522966180394361)
XLA Ops:
  0.0 3.7 %shard_map.109 = bf16[32,200,128]{2,1,0:T(8,128)(2,1)S(1)} custom-call(bf16[32,64,256]{2,1,0:T(8,128)(2,1)} %img_hbm.1, bf16[16,64,256]{2,1,0:T(8,128)(2,1)} %ref_hbm.1, s32[8,32]{1,0:T(8,128)} %bitcast.2, s32[1,32]{1,0:T(1,128)} %bitcast.3, bf16[256,256]{1,0:T(8,128)(2,1)} %constant.12.clone.fwd_hbm), custom_call_target="tpu_custom_call" | custom-call | tf_op jit(solution)/shard_map/pallas_call | solution.py:331
  3.8 0.0 copy-start
  3.8 0.0 copy-start.2
  3.8 0.0 copy-start.5
  3.8 32.0 %all_to_all.20.refs_0_ = bf16[32,200,128]{2,1,0:T(8,128)(2,1)S(1)} all-to-all(bf16[32,200,128]{2,1,0:T(8,128)(2,1)S(1)} %shard_map.109), channel_id=1, replica_groups=mesh['dom'=8,'cls'=32] {'cls'}, dimensions={0} | all-to-all | bytes 3276800 | tf_op jit(solution)/shard_map/all_to_all | solution.py:358
  35.8 0.0 copy-done
  35.8 0.0 copy-done.2
  35.8 0.0 copy-done.5
  35.8 0.0 copy-start.3
  35.9 0.0 copy-start.4
  35.9 6.5 %shard_map.110 = (f32[32,8,256]{2,1,0:T(8,128)S(1)}, f32[512,1024]{1,0:T(8,128)S(1)}, f32[512,1024]{1,0:T(8,128)S(1)}, bf16[4,512,2048]{2,1,0:T(8,128)(2,1)S(1)}, f32[64,1024]{1,0:T(8,128)S(1)}) custom-call(bf16[32,200,128]{2,1,0:T(8,128)(2,1)S(1)} %all_to_all.20.refs_0_, f32[64,64]{1,0:T(8,128)S(1)} %copy-done.5, bf16[512,512]{1,0:T(8,128)(2,1)S(1)} %copy-done.2, ...), custom_call_target="tpu_custom_call" | custom-call | tf_op jit(solution)/shard_map/pallas_call | solution.py:331
  42.4 12.5 %all_to_all.21.x_ref = f32[32,8,256]{2,1,0:T(8,128)S(1)} all-to-all(f32[32,8,256]{2,1,0:T(8,128)S(1)} %get-tuple-element.10), channel_id=1, replica_groups=mesh['dom'=8,'cls'=32] {'cls'}, dimensions={0} | all-to-all | bytes 524288 | tf_op jit(solution)/shard_map/all_to_all | solution.py:358
  54.9 0.0 copy-done.3
  54.9 0.0 copy-done.4
  54.9 1.2 %shard_map.111 = bf16[32,8,256]{2,1,0:T(8,128)(2,1)S(1)} custom-call(f32[32,8,256]{2,1,0:T(8,128)S(1)} %all_to_all.21.x_ref, f32[256,256]{1,0:T(8,128)S(1)} %copy-done.4, f32[256,256]{1,0:T(8,128)S(1)} %copy-done.3), custom_call_target="tpu_custom_call" | custom-call | tf_op jit(solution)/shard_map/pallas_call | solution.py:331
  56.0 11.2 %all_to_all.22.w_ref = bf16[32,8,256]{2,1,0:T(8,128)(2,1)S(1)} all-to-all(bf16[32,8,256]{2,1,0:T(8,128)(2,1)S(1)} %shard_map.111), channel_id=1, replica_groups=mesh['dom'=8,'cls'=32] {'cls'}, dimensions={0} | all-to-all | bytes 262144 | tf_op jit(solution)/shard_map/all_to_all | solution.py:358
  67.2 0.0 copy-start.1
  67.2 5.9 %shard_map.112 = bf16[256,2,640]{2,1,0:T(2,128)(2,1)S(1)} custom-call(bf16[32,8,256]{2,1,0:T(8,128)(2,1)S(1)} %all_to_all.22.w_ref, f32[512,1024]{1,0:T(8,128)S(1)} %get-tuple-element.11.cp_ref, f32[512,1024]{1,0:T(8,128)S(1)} %get-tuple-element.12.cq_ref, bf16[4,512,2048]{2,1,0:T(8,128)(2,1)S(1)} %get-tuple-element.13.hot_ref, ...), custom_call_target="tpu_custom_call" | custom-call | tf_op jit(solution)/shard_map/pallas_call | solution.py:331
  73.1 33.3 %all_to_all.23.in_ref = bf16[256,2,640]{2,1,0:T(2,128)(2,1)S(1)} all-to-all(bf16[256,2,640]{2,1,0:T(2,128)(2,1)S(1)} %shard_map.112), channel_id=1, replica_groups=mesh['dom'=8,'cls'=32] {'dom','cls'}, dimensions={0} | all-to-all | bytes 1310720 | tf_op jit(solution)/shard_map/all_to_all | solution.py:358
  106.4 0.0 copy-done.1
  106.4 1.3 %shard_map.113 = f32[16,8,256]{2,1,0:T(8,128)} custom-call(bf16[256,2,640]{2,1,0:T(2,128)(2,1)S(1)} %all_to_all.23.in_ref, bf16[4,256,512]{2,1,0:T(8,128)(2,1)S(1)} %copy-done.1), custom_call_target="tpu_custom_call" | custom-call | tf_op jit(solution)/shard_map/pallas_call | solution.py:331
Async XLA Ops:
  3.8 32.1 %copy-start = (bf16[1024,1024]{1,0:T(8,128)(2,1)S(1)}, bf16[1024,1024]{1,0:T(8,128)(2,1)}, u32[]{:S(2)}) copy-start(bf16[1024,1024]{1,0:T(8,128)(2,1)} %constant.14.clone.refs_3_) | copy-start | bytes 6291460
  3.8 32.1 %copy-start.2 = (bf16[512,512]{1,0:T(8,128)(2,1)S(1)}, bf16[512,512]{1,0:T(8,128)(2,1)}, u32[]{:S(2)}) copy-start(bf16[512,512]{1,0:T(8,128)(2,1)} %constant.13.clone.refs_2_) | copy-start | bytes 1572868
  3.8 32.1 %copy-start.5 = (f32[64,64]{1,0:T(8,128)S(1)}, f32[64,64]{1,0:T(8,128)}, u32[]{:S(2)}) copy-start(f32[64,64]{1,0:T(8,128)} %refs_1_.1) | copy-start | bytes 49156
  35.8 19.0 %copy-start.3 = (f32[256,256]{1,0:T(8,128)S(1)}, f32[256,256]{1,0:T(8,128)}, u32[]{:S(2)}) copy-start(f32[256,256]{1,0:T(8,128)} %constant.16.clone.fwd_ref) | copy-start | bytes 786436
  35.9 19.0 %copy-start.4 = (f32[256,256]{1,0:T(8,128)S(1)}, f32[256,256]{1,0:T(8,128)}, u32[]{:S(2)}) copy-start(f32[256,256]{1,0:T(8,128)} %constant.15.clone.inv_ref) | copy-start | bytes 786436
  67.2 39.2 %copy-start.1 = (bf16[4,256,512]{2,1,0:T(8,128)(2,1)S(1)}, bf16[4,256,512]{2,1,0:T(8,128)(2,1)}, u32[]{:S(2)}) copy-start(bf16[4,256,512]{2,1,0:T(8,128)(2,1)} %constant.17.clone.order_ref) | copy-start | bytes 3145732
